TPU v7x, 32 devices: a whole 2x2x4 slice. The times are simulated.
32 devices in a mesh: group: 4 (over z), tensor: 8 (over y, x, core).
Axes of the slice: x: 2, y: 2, z: 4, core: 2. Of those that a mesh axis runs over, the one named last changes fastest.
Arguments:
- low_state: bfloat16 [2048, 8192], P('group', 'tensor'), may hold values from -6 to 6
- mid_state: bfloat16 [2048, 8192], P('group', 'tensor'), may hold values from -6 to 6
- residual: bfloat16 [2048, 8192], P('group', 'tensor'), may hold values from -6 to 6
- attention: bfloat16 [2048, 8192], P('group', 'tensor'), may hold values from -6 to 6
- o_weight: bfloat16 [8192, 8192], P('tensor'), may hold values from -0.0625 to 0.0625
- fc_weight: bfloat16 [3, 8192, 8192], P(None, 'tensor', 'group'), may hold values from -0.0390625 to 0.0390625
- norm_gain: float32 [8192], P('group'), may hold values from 0.1 to 1.9
- target: bfloat16 [512, 8192], P('tensor', 'group'), may hold values from -6 to 6
- counts: int32 [4], replicated, may hold values from 32 to 128, as said below
- accept_rows: int32 [4, 512], replicated, may hold values from 0 to 511, each once within a row
- owners: int32 [4, 512], replicated, may hold values from 0 to 3, as said below
Outputs:
- top_state: bfloat16 [2048, 8192], P('group', 'tensor')
- fc_grad: float32 [3, 8192, 8192], P(None, 'tensor', 'group')
Inputs may be any that keep to these rules, and one draw needn't show every extreme that they name: The counts sum to exactly 256. Every replica accepts at least 32 rows, and in every draw one replica accepts 4 * 32. `accept_rows`: only the first counts[g] entries of row g are accepted rows. `owners`: among the first counts[g] entries of row g no shard appears more than 32 times; in every draw one shard receives exactly 32 rows from every replica, and the replica with the most accepted rows sends 32 to every shard. Later entries are unused.
All inputs are finite; a program needn't handle non-finite values.
Results may differ from a plain program's by a relative error of at most 0.012.
Values may be sent and summed in bfloat16 or wider, within the bound.
No kernel may reach another device: no remote copies, remote signals or barrier semaphores. Data moves between devices by JAX's collectives and lax.ppermute only.
A program may use at most 128 MiB of HBM per device.

v0:
```python
import jax
import jax.numpy as jnp
from jax import lax
from jax.sharding import PartitionSpec as P

D = 8192
SLOTS = 32


epsilon = 1e-05


def send_plan(counts, accept_rows, owners, group_count, group_index, slots):
    rows = owners.shape[1]
    live = jnp.arange(rows, dtype=jnp.int32)[None, :] < counts[:, None]
    onehot = (
        (owners[:, :, None] == jnp.arange(group_count, dtype=jnp.int32)[None, None, :])
        & live[:, :, None]
    ).astype(jnp.int32)
    mine = lax.dynamic_index_in_dim(onehot, group_index, 0, keepdims=False)
    mine_live = lax.dynamic_index_in_dim(live, group_index, 0, keepdims=False)
    mine_owner = lax.dynamic_index_in_dim(owners, group_index, 0, keepdims=False)
    mine_rows = lax.dynamic_index_in_dim(accept_rows, group_index, 0, keepdims=False)
    ranks = jnp.sum((jnp.cumsum(mine, axis=0) - mine) * mine, axis=1)
    local = jnp.where(mine_live, mine_owner * slots + ranks, -1)
    match = (local[None, :] == jnp.arange(group_count * slots, dtype=jnp.int32)[:, None]).astype(
        jnp.int32
    )
    send_index = jnp.sum(match * mine_rows[None, :], axis=1)
    send_live = jnp.sum(match, axis=1)
    per_pair = jnp.sum(onehot, axis=1)
    valid = (jnp.arange(slots, dtype=jnp.int32)[None, None, :] < per_pair.T[:, :, None]).astype(
        jnp.float32
    )
    return (send_index, send_live, valid.reshape(-1))


def row_backward(combined, target, gain, valid, total):
    squares = lax.psum(jnp.sum(combined * combined, axis=1), "group")
    scale = lax.rsqrt(squares / D + epsilon)
    normed = combined * scale[:, None] * gain[None, :]
    slope = valid[:, None] * (normed - target.astype(jnp.float32)) / total
    inner = lax.psum(jnp.sum(gain[None, :] * slope * combined, axis=1), "group")
    back = scale[:, None] * gain[None, :] * slope - combined * (scale**3 * inner / D)[:, None]
    return back.astype(jnp.bfloat16)


def shards(
    low_state,
    mid_state,
    residual,
    attention,
    o_weight,
    fc_weight,
    norm_gain,
    target,
    counts,
    accept_rows,
    owners,
):
    group_count = lax.axis_size("group")
    tensor_count = lax.axis_size("tensor")
    group_index = lax.axis_index("group")
    tensor_index = lax.axis_index("tensor")
    term = jnp.dot(attention, o_weight, preferred_element_type=jnp.float32)
    summed = lax.psum_scatter(
        term.astype(jnp.bfloat16), "tensor", scatter_dimension=1, tiled=True
    ).astype(jnp.float32)
    top_state = (residual.astype(jnp.float32) + summed).astype(jnp.bfloat16)
    send_index, send_live, valid = send_plan(
        counts, accept_rows, owners, group_count, group_index, SLOTS
    )
    states = jnp.concatenate([low_state, mid_state, top_state], axis=1)
    feature_count = states.shape[1]
    picked = jnp.take(states, send_index, axis=0) * send_live[:, None].astype(jnp.bfloat16)
    picked = picked.reshape(group_count, SLOTS, feature_count)
    everyone = lax.all_gather(picked[None], "group", axis=0, tiled=True)
    gathered = jnp.swapaxes(everyone, 0, 1).reshape(-1, feature_count)
    weights = fc_weight.reshape(feature_count, fc_weight.shape[2])
    total = jnp.sum(counts).astype(jnp.float32)
    train_rows = gathered.shape[0]
    share = train_rows // tensor_count
    block_rows = gathered
    combined = lax.psum_scatter(
        jnp.dot(block_rows, weights, preferred_element_type=jnp.float32).astype(jnp.bfloat16),
        "tensor",
        scatter_dimension=0,
        tiled=True,
    ).astype(jnp.float32)
    mine_valid = lax.dynamic_slice_in_dim(valid, tensor_index * share, share, 0)
    back = row_backward(combined, target, norm_gain, mine_valid, total)
    block_rows = gathered
    grad = lax.dot_general(
        block_rows,
        lax.all_gather(back, "tensor", axis=0, tiled=True),
        (((0,), (0,)), ((), ())),
        preferred_element_type=jnp.float32,
    )
    return (top_state, grad.reshape(fc_weight.shape))


def solution(mesh):
    in_specs = (
        P("group", "tensor"),
        P("group", "tensor"),
        P("group", "tensor"),
        P("group", "tensor"),
        P("tensor", None),
        P(None, "tensor", "group"),
        P("group"),
        P("tensor", "group"),
        P(),
        P(),
        P(),
    )
    out_specs = (P("group", "tensor"), P(None, "tensor", "group"))
    return jax.shard_map(shards, mesh=mesh, in_specs=in_specs, out_specs=out_specs, check_vma=False)
```

profile of v0, /device:TPU:0, one launch (start us, length us, event | category | flops | bytes accessed | tf_op | source)
XLA Modules:
  0.0 295.1 jit_solution(10319330807158271678)
XLA Ops:
  7.2 1.2 copy-done
  8.4 16.8 %convolution_convert_fusion = bf16[512,8192]{1,0:T(8,128)(2,1)} fusion(bf16[512,1024]{1,0:T(8,128)(2,1)S(1)} %copy-done, bf16[1024,8192]{1,0:T(8,128)(2,1)} %param.15), kind=kOutput, calls=%fused_computation.1 | convolution fusion | flops 8594128896 | bytes 26214400 | tf_op jit(solution)/shard_map/dot_general | solution.py:65
  25.3 0.6 copy-done.8
  26.0 1.2 reduce-window.6
  27.2 0.2 slice_reduce_fusion
  27.7 0.7 dynamic-slice_select_fusion
  28.7 70.7 %reduce-scatter.3.cloned.1.call-done = bf16[512,1024]{1,0:T(8,128)(2,1)} async-done(((bf16[512,8192]{1,0:T(8,128)(2,1)}), bf16[512,1024]{1,0:T(8,128)(2,1)}) %reduce-scatter.3.cloned.1.call-update) | async-done | bytes 1048592 | tf_op jit(solution)/shard_map/reduce_scatter | solution.py:66
  99.4 1.6 add_convert_fusion
  101.0 1.0 copy-done.2
  102.0 1.7 pad_maximum_fusion
  103.7 1.9 gather_fusion
  105.6 2.2 select_multiply_fusion
  107.8 63.5 %all-gather.3.cloned.1.call-done = bf16[4,4,32,3072]{3,2,0,1:T(8,128)(2,1)} async-done(((bf16[1,4,32,3072]{3,2,0,1:T(8,128)(2,1)}), bf16[4,4,32,3072]{3,2,0,1:T(8,128)(2,1)}) %all-gather.3.cloned.1.call-update) | async-done | bytes 3145744 | tf_op jit(solution)/shard_map/all_gather | solution.py:77
  171.4 11.6 %convolution_convert_fusion.1 = bf16[512,2048]{1,0:T(8,128)(2,1)} fusion(bf16[512,3072]{1,0:T(8,128)(2,1)} %bitcast.43, bf16[3072,2048]{1,0:T(8,128)(2,1)} %bitcast.51), kind=kOutput, calls=%fused_computation.3 | convolution fusion | flops 6443499520 | bytes 17825792 | tf_op jit(solution)/shard_map/dot_general | solution.py:85
  183.0 0.6 reduce_sum.77
  184.9 37.9 %reduce-scatter.5.cloned.1.call-done = bf16[64,2048]{1,0:T(8,128)(2,1)} async-done(((bf16[512,2048]{1,0:T(8,128)(2,1)}), bf16[64,2048]{1,0:T(8,128)(2,1)}) %reduce-scatter.5.cloned.1.call-update) | async-done | bytes 262160 | tf_op jit(solution)/shard_map/reduce_scatter | solution.py:84
  222.9 1.1 fusion.2
  224.0 11.7 %psum.14 = f32[64]{0:T(128)S(1)} all-reduce(f32[64]{0:T(128)S(1)} %fusion.2), channel_id=1, replica_groups=mesh['group'=4,'tensor'=8] {'group'}, use_global_device_ids=true, to_apply=%region_8.9 | all-reduce | flops 64 | bytes 512 | tf_op jit(solution)/shard_map/psum | solution.py:39
  235.7 1.3 fusion.7
  237.0 8.4 %psum.15 = f32[64]{0:T(128)S(1)} all-reduce(f32[64]{0:T(128)S(1)} %fusion.7), channel_id=1, replica_groups=mesh['group'=4,'tensor'=8] {'group'}, use_global_device_ids=true, to_apply=%region_12.13 | all-reduce | flops 64 | bytes 512 | tf_op jit(solution)/shard_map/psum | solution.py:43
  245.4 2.0 fusion.9
  247.4 2.8 copy.20
  250.3 23.8 %all-gather.5.cloned.1.call-done = bf16[512,2048]{1,0:T(8,128)(2,1)} async-done(((bf16[64,2048]{1,0:T(8,128)(2,1)}), bf16[512,2048]{1,0:T(8,128)(2,1)}) %all-gather.5.cloned.1.call-update) | async-done | bytes 2097168 | tf_op jit(solution)/shard_map/all_gather | solution.py:95
  274.0 14.5 %fusion = f32[3,1024,2048]{2,1,0:T(8,128)} fusion(bf16[3,1024,512]{2,1,0:T(8,128)(2,1)} %bitcast.45, bf16[512,2048]{1,0:T(8,128)(2,1)} %all-gather.5.cloned.1.call-done), kind=kOutput, calls=%fused_computation.4 | convolution fusion | flops 6442450944 | bytes 30408704 | tf_op jit(solution)/shard_map/dot_general | solution.py:93
  (44 shorter events, 1.5 us)
Async XLA Ops:
  7.2 1.2 copy-start
  7.2 92.2 %reduce-scatter.3.cloned.1.call-start = ((), (), s32[]{:S(2)}) async-start(), calls=%async_computation.2 | async-start | bytes 9437184 | tf_op jit(solution)/shard_map/reduce_scatter | solution.py:66
  25.2 0.7 copy-start.8
  25.2 0.7 copy-start.6
  25.2 74.2 %copy-start.4 = (bf16[512,1024]{1,0:T(8,128)(2,1)S(1)}, bf16[512,1024]{1,0:T(8,128)(2,1)}, u32[]{:S(2)}) copy-start(bf16[512,1024]{1,0:T(8,128)(2,1)} %param.13) | copy-start | bytes 3145732
  25.2 146.2 %all-gather.3.cloned.1.call-start = ((), (), s32[]{:S(2)}) async-start(), calls=%async_computation.3 | async-start | bytes 3932160 | tf_op jit(solution)/shard_map/all_gather | solution.py:77
  101.0 1.0 copy-start.2
  107.8 115.1 %reduce-scatter.5.cloned.1.call-start = ((), (), s32[]{:S(2)}) async-start(), calls=%async_computation.4 | async-start | bytes 2359296 | tf_op jit(solution)/shard_map/reduce_scatter | solution.py:84
  171.4 64.3 %copy-start.5 = (bf16[64,2048]{1,0:T(8,128)(2,1)S(1)}, bf16[64,2048]{1,0:T(8,128)(2,1)}, u32[]{:S(2)}) copy-start(bf16[64,2048]{1,0:T(8,128)(2,1)} %param.18) | copy-start | bytes 786436
  171.4 64.3 %copy-start.7 = (f32[2048]{0:T(1024)S(1)}, f32[2048]{0:T(1024)}, u32[]{:S(2)}) copy-start(f32[2048]{0:T(1024)} %param.17) | copy-start | bytes 24580
  182.9 64.5 %copy-start.3 = (bf16[4,4,32,3072]{3,2,0,1:T(8,128)(2,1)S(1)}, bf16[4,4,32,3072]{3,2,0,1:T(8,128)(2,1)}, u32[]{:S(2)}) copy-start(bf16[4,4,32,3072]{3,2,0,1:T(8,128)(2,1)} %all-gather.3.cloned.1.call-done) | copy-start | bytes 9437188
  183.0 91.1 %all-gather.5.cloned.1.call-start = ((), (), s32[]{:S(2)}) async-start(), calls=%async_computation.5 | async-start | bytes 2359296 | tf_op jit(solution)/shard_map/all_gather | solution.py:95
  274.0 14.5 %copy-start.1 = (bf16[512,1024]{1,0:T(8,128)(2,1)S(1)}, bf16[512,1024]{1,0:T(8,128)(2,1)}, u32[]{:S(2)}) copy-start(bf16[512,1024]{1,0:T(8,128)(2,1)} %param.14) | copy-start | bytes 3145732
Sparse Core Ops, SparseCore 0:
  25.3 74.0 reduce-scatter.2
  107.9 63.4 all-gather.2
  183.1 39.7 reduce-scatter.4
  247.6 26.4 all-gather.4
where the time goes:
time: 296 us; the launch traced here: 295 us
  waiting for transfers between devices  196 us (66%)
  matrix products  42.8 us (14%)
  blocking collectives  20.1 us (7%)
  between operations  14.7 us (5%)
  other arithmetic  13.2 us (4%)
  local copies, waits for them, and re-layouts  8.15 us (3%)
    reduce_scatter x1, waiting for transfers between devices, shards(): lax.psum_scatter(term.astype(jnp.bfloat16), 'tensor', scatter_dimension=1...  70.7 us
    all_gather x1, waiting for transfers between devices, shards(): everyone = lax.all_gather(picked[None], 'group', axis=0, tiled=True)  63.5 us
    reduce_scatter x1, waiting for transfers between devices, shards(): lax.psum_scatter(jnp.dot(block_rows, weights, preferred_element_type=jnp....  37.9 us
    all_gather x1, waiting for transfers between devices, shards(): lax.all_gather(back, 'tensor', axis=0, tiled=True)  23.8 us
    dot_general x1, matrix products, shards(): term = jnp.dot(attention, o_weight, preferred_element_type=jnp.float32)  16.8 us
    dot_general x1, matrix products, shards(): lax.dot_general(block_rows, lax.all_gather(back, 'tensor', axis=0, tiled=...  14.5 us
    psum x1, blocking collectives, row_backward(): squares = lax.psum(jnp.sum(combined * combined, axis=1), 'group')  11.7 us
    dot_general x1, matrix products, shards(): jnp.dot(block_rows, weights, preferred_element_type=jnp.float32)  11.6 us
  transfers between devices with their start and end apart: 4, of which 4 were waited for; matrix products, arithmetic and copies ran while one was open for 2% of the time, Pallas kernels for 0%

commit v1 on v0

v1 whole, which is shorter than its diff:
```python
import functools

import jax
import jax.numpy as jnp
from jax import lax
from jax.experimental import pallas as pl
from jax.experimental.pallas import tpu as pltpu
from jax.sharding import PartitionSpec as P


epsilon = 1e-05
f32 = jnp.float32
bf16 = jnp.bfloat16
i32 = jnp.int32


VMEM = pl.BlockSpec(memory_space=pltpu.VMEM)
SMEM = pl.BlockSpec(memory_space=pltpu.SMEM)
HBM = pl.BlockSpec(memory_space=pltpu.HBM)


def iota(shape, dim):
    return lax.broadcasted_iota(i32, shape, dim)


def cost(flops, read):
    return pl.CostEstimate(flops=int(flops), bytes_accessed=int(read), transcendentals=0)


def params(mib=56):
    return pltpu.CompilerParams(vmem_limit_bytes=mib << 20)


def in_hbm(*arrays):
    return [pltpu.with_memory_space_constraint(x, pltpu.HBM) for x in arrays]


def fetch_all(pairs, sems):
    copies = [
        pltpu.make_async_copy(src, dst, sems.at[i]) for i, (src, dst) in enumerate(pairs)
    ]
    for copy in copies:
        copy.start()
    return copies


def hit(cond):
    return jnp.where(cond, 1.0, 0.0).astype(bf16)


def place_of(rows_ref, lo, hi, replica):
    groups, rows = rows_ref.shape
    ids = jnp.where(iota((groups, hi - lo), 0) == replica, rows_ref[:, lo:hi], 0)
    ids = jnp.sum(ids, axis=0, keepdims=True)
    return hit(iota((rows, hi - lo), 0) == ids)


def pick_rows(place, x):
    return lax.dot_general(
        place, x, (((0,), (0,)), ((), ())), preferred_element_type=f32
    ).astype(bf16)


def early_kernel(rows_ref, low_ref, mid_ref, *refs):
    *outs, ids, buf, sem = refs
    copies = fetch_all([(rows_ref, ids), (low_ref, buf.at[0]), (mid_ref, buf.at[1])], sem)
    copies[0].wait()
    place = place_of(ids, 0, outs[0].shape[1], lax.axis_index("group"))
    for i in range(2):
        copies[1 + i].wait()
        got = pick_rows(place, buf[i])
        for out in outs:
            out[i] = got[: out.shape[1]]


def early_rows(accept_rows, low, mid, common, cap):
    rows, width = low.shape
    shapes = [(2, cap, width)] + ([(2, common, width)] if cap > common else [])
    return pl.pallas_call(
        early_kernel,
        in_specs=[HBM] * 3,
        out_specs=[VMEM] * len(shapes),
        out_shape=[jax.ShapeDtypeStruct(s, bf16) for s in shapes],
        scratch_shapes=[
            pltpu.VMEM(accept_rows.shape, i32),
            pltpu.VMEM((2, rows, width), bf16),
            pltpu.SemaphoreType.DMA((3,)),
        ],
        compiler_params=params(8),
        cost_estimate=cost(4 * rows * width * cap, 4 * rows * width + 4 * cap * width),
        name="early_rows",
    )(*in_hbm(accept_rows, low, mid))


def project_kernel(
    chip_order,
    cap,
    rows_ref,
    att_ref,
    res_ref,
    w_ref,
    give_acc,
    keep_acc,
    res_acc,
    give_rest,
    keep_rest,
    res_rest,
    ids,
    att,
    res,
    picked,
    wbuf,
    obuf,
    sem,
    small_sem,
):
    chips = len(chip_order)
    width = wbuf.shape[2]
    rows = att.shape[0]
    t = lax.axis_index("tensor")

    def fetch(i, block):
        at = pl.ds(pl.multiple_of((t ^ block) * width, 128), width)
        return pltpu.make_async_copy(w_ref.at[:, at], wbuf.at[i], sem.at[0, i])

    def put(i):
        j = i % chips
        rest = give_rest if i < chips else keep_rest
        copies = [
            pltpu.make_async_copy(
                obuf.at[i, pl.ds(cap, rows - cap)], rest.at[j], sem.at[1, i]
            )
        ]
        if i < chips:
            copies.append(
                pltpu.make_async_copy(
                    obuf.at[i, pl.ds(0, cap)], give_acc.at[j], sem.at[2, i]
                )
            )
        return copies

    order = [2 * m + 1 for m in chip_order] + [2 * m for m in chip_order]
    ahead = 3
    copies = fetch_all([(rows_ref, ids), (att_ref, att)], small_sem)
    late = pltpu.make_async_copy(res_ref, res, small_sem.at[2])
    for i in range(ahead):
        fetch(i, order[i]).start()
    copies[0].wait()
    place = place_of(ids, 0, rows, lax.axis_index("group"))
    copies[1].wait()
    x = pick_rows(place, att[...])
    for i, block in enumerate(order):
        fetch(i, block).wait()
        if i + ahead < len(order):
            fetch(i + ahead, order[i + ahead]).start()
        elif i + ahead == len(order):
            late.start()
        y = jnp.dot(x, wbuf[i], preferred_element_type=f32).astype(bf16)
        obuf[i] = y
        if i >= chips:
            keep_acc[i - chips] = y[:cap]
        for copy in put(i):
            copy.start()
    late.wait()
    picked[...] = pick_rows(place, res[...])
    res_acc[...] = picked[:cap]
    last = pltpu.make_async_copy(picked.at[pl.ds(cap, rows - cap)], res_rest, small_sem.at[3])
    last.start()
    for i in range(2 * chips):
        for copy in put(i):
            copy.wait()
    last.wait()


def project(accept_rows, attention, residual, o_weight, chip_order, cap, width):
    rows, depth = attention.shape
    chips = len(chip_order)
    acc, rest = (chips, cap, width), (chips, rows - cap, width)
    return pl.pallas_call(
        functools.partial(project_kernel, chip_order, cap),
        in_specs=[HBM] * 4,
        out_specs=[HBM, VMEM, VMEM, HBM, HBM, HBM],
        out_shape=[
            pltpu.HBM(acc, bf16),
            jax.ShapeDtypeStruct(acc, bf16),
            jax.ShapeDtypeStruct(acc[1:], bf16),
            pltpu.HBM(rest, bf16),
            pltpu.HBM(rest, bf16),
            pltpu.HBM(rest[1:], bf16),
        ],
        scratch_shapes=[
            pltpu.VMEM(accept_rows.shape, i32),
            pltpu.VMEM(attention.shape, bf16),
            pltpu.VMEM(residual.shape, bf16),
            pltpu.VMEM(residual.shape, bf16),
            pltpu.VMEM((2 * chips, depth, width), bf16),
            pltpu.VMEM((2 * chips, rows, width), bf16),
            pltpu.SemaphoreType.DMA((3, 2 * chips)),
            pltpu.SemaphoreType.DMA((4,)),
        ],
        compiler_params=params(36),
        cost_estimate=cost(
            4 * rows * depth * width * chips, 4 * depth * width * chips + 4 * rows * width * chips
        ),
        name="project",
    )(*in_hbm(accept_rows, attention, residual, o_weight))


def pair_sums(keep, got, res):
    chips, rows, width = keep.shape

    def kernel(keep_ref, got_ref, res_ref, own_out, *outs):
        own_out[...] = (
            res_ref[...].astype(f32) + keep_ref[0].astype(f32) + got_ref[0].astype(f32)
        )
        for i, out in enumerate(outs):
            out[...] = (keep_ref[i + 1].astype(f32) + got_ref[i + 1].astype(f32)).astype(bf16)

    return pl.pallas_call(
        kernel,
        in_specs=[VMEM] * 3,
        out_specs=[VMEM] * chips,
        out_shape=[jax.ShapeDtypeStruct((rows, width), f32)]
        + [jax.ShapeDtypeStruct((rows, width), bf16)] * (chips - 1),
        compiler_params=params(8),
        cost_estimate=cost(chips * rows * width, 6 * chips * rows * width),
        name="pair_sums",
    )(keep, got, res)


def top_rows(own, came, first):
    rows, width = own.shape
    shapes = [(1, rows, width)] + ([(1, first, width)] if rows > first else [])

    def kernel(own_ref, *refs):
        total = own_ref[...]
        for ref in refs[: len(came)]:
            total = total + ref[...].astype(f32)
        for out in refs[len(came) :]:
            out[0] = total[: out.shape[1]].astype(bf16)

    return pl.pallas_call(
        kernel,
        in_specs=[VMEM] * (1 + len(came)),
        out_specs=[VMEM] * len(shapes),
        out_shape=[jax.ShapeDtypeStruct(s, bf16) for s in shapes],
        compiler_params=params(8),
        cost_estimate=cost(4 * rows * width, 12 * rows * width),
        name="top_rows",
    )(own, *came)


def start_of(counts_ref, replica):
    total = jnp.int32(0)
    for s in range(counts_ref.shape[0]):
        total = total + jnp.where(s < replica, counts_ref[s], 0)
    return total


def busiest_of(counts_ref):
    best, where = counts_ref[0], jnp.int32(0)
    for s in range(1, counts_ref.shape[0]):
        more = counts_ref[s] > best
        best = jnp.where(more, counts_ref[s], best)
        where = jnp.where(more, jnp.int32(s), where)
    return where


def rows_here(accepted, columns):
    p = iota((accepted, columns), 0) + (lax.axis_index("tensor") % 2) * (accepted // 2)
    return jnp.where(p >= accepted, p - accepted, p)


def destination(counts_ref, replica, k):
    return jnp.where(k < counts_ref[replica], start_of(counts_ref, replica) + k, -1)


def join_call(counts, gathered, extra, weight, so_far, common, cap, accepted):
    groups = len(gathered)
    thirds, _, width = gathered[0].shape
    features = weight.shape[-1]
    half = accepted // 2
    has_extra = extra is not None
    final = so_far is not None
    columns = groups * common + (cap - common if has_extra else 0)

    def kernel(counts_ref, *refs):
        refs = list(refs)
        blocks = [refs.pop(0) for _ in range(groups + has_extra)]
        so_far_ref = refs.pop(0) if final else None
        w_ref = refs.pop(0)
        rows_out = refs.pop(0)
        if final:
            *outs, joined = refs
            weights = [w_ref]
        else:
            *outs, joined, wbuf, wsem = refs
            weights = [wbuf.at[i] for i in range(thirds)]
            landing = weights + [outs[1]]
            copies = [
                pltpu.make_async_copy(w_ref.at[i], ref, wsem.at[i])
                for i, ref in enumerate(landing)
            ]
            copies[0].start()
            copies[1].start()
        g = lax.axis_index("group")
        j = iota((8, columns), 1)
        goes = jnp.full((8, columns), -1, i32)
        for back in range(groups):
            replica = g ^ back
            inside = (j >= back * common) & (j < (back + 1) * common)
            goes = jnp.where(inside, destination(counts_ref, replica, j - back * common), goes)
        if has_extra:
            k = j - groups * common + common
            goes = jnp.where(
                j >= groups * common, destination(counts_ref, busiest_of(counts_ref), k), goes
            )
        place = hit(rows_here(accepted, columns) == goes[:1])
        total = so_far_ref[...] if final else None
        for i in range(thirds):
            for back in range(groups):
                joined[i, back * common : (back + 1) * common] = blocks[back][i, :common]
            if has_extra:
                joined[i, groups * common :] = blocks[groups][i]
            x = jnp.dot(place, joined[i], preferred_element_type=f32).astype(bf16)
            rows_out[i] = x
            if not final:
                copies[i].wait()
                if i == 0:
                    copies[thirds].start()
            y = jnp.dot(x, weights[i][...], preferred_element_type=f32)
            total = y if total is None else total + y
        if final:
            outs[0][...] = total[:half]
            outs[1][...] = total[half:].astype(bf16)
        else:
            outs[0][...] = total
            copies[thirds].wait()

    rows_shape = jax.ShapeDtypeStruct((thirds, accepted, width), bf16)
    if final:
        out_shape = [
            rows_shape,
            jax.ShapeDtypeStruct((half, features), f32),
            jax.ShapeDtypeStruct((half, features), bf16),
        ]
    else:
        out_shape = [
            rows_shape,
            jax.ShapeDtypeStruct((accepted, features), f32),
            jax.ShapeDtypeStruct((width, features), bf16),
        ]
    operands = [counts, *gathered]
    if has_extra:
        operands.append(extra)
    if final:
        operands.append(so_far)
    return pl.pallas_call(
        kernel,
        in_specs=[SMEM] + [VMEM] * (len(operands) - 1) + [VMEM if final else HBM],
        out_specs=[VMEM] * len(out_shape),
        out_shape=out_shape,
        scratch_shapes=[pltpu.VMEM((thirds, columns, width), bf16)]
        + (
            []
            if final
            else [
                pltpu.VMEM((thirds, width, features), bf16),
                pltpu.SemaphoreType.DMA((thirds + 1,)),
            ]
        ),
        compiler_params=params(12 if final else 20),
        cost_estimate=cost(
            2 * thirds * accepted * width * features, 2 * thirds * width * features
        ),
        name="join_late" if final else "join_early",
    )(*operands, weight if final else in_hbm(weight)[0])


def goal_kernel(slots, cap, accepted, counts_ref, owners_ref, *refs):
    *sources, mine_out, other_out, held_targets, sem = refs
    targets = [held_targets.at[m] for m in range(len(sources))]
    copies = [
        pltpu.make_async_copy(ref, held_targets.at[m], sem.at[m])
        for m, ref in enumerate(sources)
    ]
    for copy in copies:
        copy.start()
    groups = owners_ref.shape[0]
    share = targets[0].shape[0]
    half = accepted // 2
    t = lax.axis_index("tensor")
    before = hit(iota((cap, cap), 0) < iota((cap, cap), 1))
    picks = [None] * len(targets)
    for g in range(groups):
        own = owners_ref[g : g + 1, :cap]
        mark = hit(iota((max(groups, 8), cap), 0) == own)
        prefix = jnp.dot(mark, before, preferred_element_type=f32)
        rank = jnp.sum(prefix * mark.astype(f32), axis=0, keepdims=True).astype(i32)
        slot = own * cap + g * slots + rank
        goes = destination(counts_ref, g, iota((8, cap), 1))
        place = hit(rows_here(accepted, cap) == goes[:1])
        for m in range(len(targets)):
            held = iota((share, cap), 0) + (t ^ (2 * m)) * share
            z = lax.dot_general(
                place, hit(held == slot), (((1,), (1,)), ((), ())), preferred_element_type=f32
            )
            picks[m] = z if picks[m] is None else picks[m] + z
    total = None
    for m, ref in enumerate(targets):
        copies[m].wait()
        y = jnp.dot(picks[m].astype(bf16), ref[...], preferred_element_type=f32)
        total = y if total is None else total + y
    mine_out[...] = total[:half].astype(bf16)
    other_out[...] = total[half:].astype(bf16)


def goals(counts, owners, targets, slots, cap, accepted):
    features = targets[0].shape[1]
    return pl.pallas_call(
        functools.partial(goal_kernel, slots, cap, accepted),
        in_specs=[SMEM, VMEM] + [HBM] * len(targets),
        out_specs=[VMEM, VMEM],
        out_shape=[jax.ShapeDtypeStruct((accepted // 2, features), bf16)] * 2,
        scratch_shapes=[
            pltpu.VMEM((len(targets),) + targets[0].shape, bf16),
            pltpu.SemaphoreType.DMA((len(targets),)),
        ],
        compiler_params=params(28),
        cost_estimate=cost(2 * accepted * accepted * features, 4 * accepted * features),
        name="goals",
    )(counts, owners, *in_hbm(*targets))


def gauge(pieces, arrived, goal, goal_came, gain):
    half, part = pieces[0].shape
    n = len(pieces)
    features = part * n

    def kernel(*refs):
        piece_refs, came_refs = refs[:n], refs[n : 2 * n]
        goal_ref, goal_came_ref, gain_ref, c_out, goal_out, stats_out = refs[2 * n :]
        sums = [0.0, 0.0, 0.0]
        for i in range(n):
            at = slice(i * part, (i + 1) * part)
            c = piece_refs[i][...] + came_refs[i][...].astype(f32)
            goal = goal_ref[:, at].astype(f32) + goal_came_ref[:, at].astype(f32)
            gc = gain_ref[:, at] * c
            c_out[:, at] = c
            goal_out[:, at] = goal
            for k, v in enumerate((c * c, gc * gc, gc * goal)):
                sums[k] = sums[k] + jnp.sum(v, axis=1, keepdims=True)
        lane = iota((half, 128), 1)
        stats = jnp.zeros((half, 128), f32)
        for k in range(3):
            stats = jnp.where(lane == k, sums[k], stats)
        stats_out[...] = stats.T[:8]

    whole = jax.ShapeDtypeStruct((half, features), f32)
    return pl.pallas_call(
        kernel,
        in_specs=[VMEM] * (2 * n + 3),
        out_specs=[VMEM] * 3,
        out_shape=[whole, whole, jax.ShapeDtypeStruct((8, half), f32)],
        compiler_params=params(16),
        cost_estimate=cost(10 * half * features, 20 * half * features),
        name="gauge",
    )(*pieces, *arrived, goal, goal_came, gain)


def backward(counts, c, goal, gain, stats, width):
    half, features = c.shape
    n = len(stats)

    def kernel(counts_ref, c_ref, goal_ref, gain_ref, *refs):
        total = counts_ref[0]
        for s in range(1, counts_ref.shape[0]):
            total = total + counts_ref[s]
        inverse = 1.0 / jnp.full((half, 1), total, i32).astype(f32)
        sums = refs[0][...]
        for ref in refs[1:n]:
            sums = sums + ref[...]
        sums = jnp.concatenate([sums, jnp.zeros((120, half), f32)], axis=0).T
        squares, gained, crossed = sums[:, 0:1], sums[:, 1:2], sums[:, 2:3]
        scale = lax.rsqrt(squares / width + epsilon)
        inner = (scale * gained - crossed) * inverse
        gain = gain_ref[...]
        c = c_ref[...]
        slope = (c * scale * gain - goal_ref[...]) * inverse
        out = scale * gain * slope - c * (scale * scale * scale * inner / width)
        refs[n][...] = out.astype(bf16)

    return pl.pallas_call(
        kernel,
        in_specs=[SMEM] + [VMEM] * (3 + n),
        out_specs=VMEM,
        out_shape=jax.ShapeDtypeStruct((half, features), bf16),
        compiler_params=params(16),
        cost_estimate=cost(10 * half * features, 10 * half * features),
        name="backward",
    )(counts, c, goal, gain, *stats)


def finish(accept_rows, top_acc, base, arrivals, early_c, late_c, back, other):
    cap, width = top_acc.shape
    rows = accept_rows.shape[1]
    accepted = early_c.shape[1]
    half, features = back.shape
    thirds = early_c.shape[0] + late_c.shape[0]
    arrays = [array for part in arrivals for array, _ in part]
    block = min(256, width)
    per = width // block
    slots = 4

    def kernel(rows_ref, acc_ref, base_ref, *refs):
        refs = list(refs)
        came = [refs.pop(0) for _ in arrays]
        early_ref, late_ref, back_ref, other_ref, top_out, grad_out = refs[:6]
        backs, obuf, sem = refs[6:]
        backs[:half] = back_ref[...]
        backs[half:] = other_ref[...]

        def put(n):
            third, b = divmod(n, per)
            return pltpu.make_async_copy(
                obuf.at[n % slots],
                grad_out.at[third, pl.ds(b * block, block)],
                sem.at[n % slots],
            )

        steps = thirds * per
        for n in range(steps):
            third, b = divmod(n, per)
            ref = early_ref.at[third] if third < early_c.shape[0] else late_ref.at[0]
            if n >= slots:
                put(n - slots).wait()
            obuf[n % slots] = lax.dot_general(
                ref[:, b * block : (b + 1) * block],
                backs[...],
                (((0,), (0,)), ((), ())),
                preferred_element_type=f32,
            )
            put(n).start()
        place = place_of(rows_ref, 0, rows, lax.axis_index("group"))
        y = jnp.dot(place[:, :cap], acc_ref[...], preferred_element_type=f32)
        at = cap
        came = iter(came)
        for part in arrivals:
            size = part[0][0].shape[1]
            v = base_ref[at - cap : at - cap + size]
            for _, i in part:
                v = v + next(came)[i].astype(f32)
            y = y + jnp.dot(
                place[:, at : at + size], v.astype(bf16), preferred_element_type=f32
            )
            at += size
        top_out[...] = y.astype(bf16)
        for n in range(max(0, steps - slots), steps):
            put(n).wait()

    return pl.pallas_call(
        kernel,
        in_specs=[VMEM] * (7 + len(arrays)),
        out_specs=[VMEM, HBM],
        out_shape=[
            jax.ShapeDtypeStruct((rows, width), bf16),
            jax.ShapeDtypeStruct((thirds, width, features), f32),
        ],
        scratch_shapes=[
            pltpu.VMEM((accepted, features), bf16),
            pltpu.VMEM((slots, block, features), f32),
            pltpu.SemaphoreType.DMA((slots,)),
        ],
        compiler_params=params(24),
        cost_estimate=cost(
            2 * accepted * thirds * width * features, 4 * thirds * width * features
        ),
        name="finish",
    )(accept_rows, top_acc, base, *arrays, early_c, late_c, back, other)


def shards(
    low_state,
    mid_state,
    residual,
    attention,
    o_weight,
    fc_weight,
    norm_gain,
    target,
    counts,
    accept_rows,
    owners,
):
    groups = lax.axis_size("group")
    tensors = lax.axis_size("tensor")
    g = lax.axis_index("group")
    chips = tensors // 2
    rows, width = low_state.shape
    out_features = fc_weight.shape[2]
    train_rows = target.shape[0] * tensors
    slots = train_rows // (groups * groups)
    cap = groups * slots
    accepted = train_rows // 2
    common = min(cap, accepted - cap - (groups - 2) * slots)
    bits = [1 << i for i in range(1, tensors.bit_length() - 1)]
    group_bits = [1 << i for i in range(groups.bit_length() - 1)]

    def swap(x, mask):
        return lax.ppermute(x, "tensor", [(i, i ^ mask) for i in range(tensors)])

    def cross(x, mask):
        return lax.ppermute(x, "group", [(i, i ^ mask) for i in range(groups)])

    busiest = jnp.argmax(counts).astype(i32)

    def gather(full, first):
        blocks = [full, cross(full, 1)]
        blocks += [cross(first, mask) for mask in range(2, groups)]
        if cap == common:
            return blocks, None
        extra = jnp.where(
            ((busiest ^ g) & 1) != 0, blocks[1][:, common:], full[:, common:]
        )
        for bit in group_bits[1:]:
            other = cross(extra, bit)
            extra = jnp.where(((busiest ^ g) & bit) != 0, other, extra)
        return blocks, extra

    early = early_rows(accept_rows, low_state, mid_state, common, cap)
    early_all, early_extra = gather(early[0], early[-1])

    targets = [target] + [swap(target, 2 * m) for m in range(1, chips)]

    gray = [i ^ (i >> 1) for i in range(chips)]
    at = {m: i for i, m in enumerate(gray)}
    give_acc, keep_acc, res_acc, give_rest, keep_rest, res_rest = project(
        accept_rows, attention, residual, o_weight, gray, cap, width
    )
    got_acc = swap(give_acc, 1)
    got_rest = swap(give_rest, 1)

    own, *others = pair_sums(keep_acc, got_acc, res_acc)
    came = [swap(others[i - 1], 2 * gray[i]) for i in range(1, chips)]
    late = top_rows(own, came, common)
    top_acc = late[0][0]
    late_all, late_extra = gather(late[0], late[-1])

    n_rest = rows - cap
    base = res_rest.astype(f32) + keep_rest[0].astype(f32) + got_rest[0].astype(f32)
    arrivals = []
    for part, order in enumerate((bits, bits[::-1])):
        lo, hi = part * (n_rest // 2), (part + 1) * (n_rest // 2)
        arrived = {m: [] for m in range(chips)}

        def value(ms):
            ps = [at[m] for m in ms]
            if not any(arrived[m] for m in ms) and ps == list(range(ps[0], ps[0] + len(ps))):
                a = slice(ps[0], ps[0] + len(ps))
                return keep_rest[a, lo:hi].astype(f32) + got_rest[a, lo:hi].astype(f32)
            vals = []
            for m in ms:
                v = keep_rest[at[m], lo:hi].astype(f32) + got_rest[at[m], lo:hi].astype(f32)
                for array, i in arrived[m]:
                    v = v + array[i].astype(f32)
                vals.append(v)
            return jnp.stack(vals)

        held = list(range(chips))
        for bit in order:
            going = sorted((m for m in held if 2 * m & bit), key=lambda m: at[m])
            sent = value(going).astype(bf16)
            came = swap(sent, bit)
            for i, m in enumerate(going):
                arrived[m ^ (bit >> 1)].append((came, i))
            held = [m for m in held if not 2 * m & bit]
        arrivals.append(arrived[0])

    early_c, partial, late_weight = join_call(
        counts, early_all, early_extra, fc_weight, None, common, cap, accepted
    )
    late_c, mine, other = join_call(
        counts, late_all, late_extra, late_weight, partial, common, cap, accepted
    )

    goal, goal_other = goals(counts, owners, targets, slots, cap, accepted)
    goal_came = swap(goal_other, 1)

    mine = mine + swap(other, 1).astype(f32)
    pieces, arrived = [], []
    for part, order in enumerate((bits, bits[::-1])):
        lo = part * (out_features // 2)
        piece = mine[:, lo : lo + out_features // 2]
        for step, bit in enumerate(order):
            came = swap(piece.astype(bf16), bit)
            if step < len(order) - 1:
                piece = piece + came.astype(f32)
        pieces.append(piece)
        arrived.append(came)

    gain = norm_gain.astype(f32)[None, :]
    c, goal, stats = gauge(pieces, arrived, goal, goal_came, gain)
    all_stats = [stats] + [cross(stats, mask) for mask in range(1, groups)]
    back = backward(counts, c, goal, gain, all_stats, out_features * groups)
    other = swap(back, 1)
    top_state, grad = finish(
        accept_rows, top_acc, base, arrivals, early_c, late_c, back, other
    )
    return (top_state, grad)


def solution(mesh):
    in_specs = (
        P("group", "tensor"),
        P("group", "tensor"),
        P("group", "tensor"),
        P("group", "tensor"),
        P("tensor", None),
        P(None, "tensor", "group"),
        P("group"),
        P("tensor", "group"),
        P(),
        P(),
        P(),
    )
    out_specs = (P("group", "tensor"), P(None, "tensor", "group"))

    return jax.shard_map(shards, mesh=mesh, in_specs=in_specs, out_specs=out_specs, check_vma=False)
```

time: 296 us -> 173 us (0.58)
  waiting for transfers between devices: 196 us -> 86 us
  matrix products: 42.8 us -> 0 us
  Pallas kernels: 0 us -> 41.4 us
  starting transfers between devices: 0.16 us -> 36.3 us
  blocking collectives: 20.1 us -> 0 us
  between operations: 14.7 us -> 1.7 us
  local copies, waits for them, and re-layouts: 8.15 us -> 0.81 us
  other arithmetic: 13.2 us -> 6.4 us
    reduce_scatter x2 -> x0, waiting for transfers between devices: 109 us -> none  [the longest x1 70.7 us: shards(): lax.psum_scatter(term.astype(jnp.bfloat16), 'tensor', scatter_dimension=1...]
    all_gather x2 -> x0, waiting for transfers between devices: 87.3 us -> none  [the longest x1 63.5 us: shards(): everyone = lax.all_gather(picked[None], 'group', axis=0, tiled=True)]
    ppermute x0 -> x30, waiting for transfers between devices: none -> 86 us  [the longest x11 48.3 us: cross(): return lax.ppermute(x, 'group', [(i, i ^ mask) for i in range(groups)])]
    dot_general x3 -> x0, matrix products: 42.8 us -> none  [the longest x1 16.8 us: shards(): term = jnp.dot(attention, o_weight, preferred_element_type=jnp.float32)]
    pallas_call x0 -> x10, Pallas kernels: none -> 41.4 us  [the longest x1 15.2 us: project(): pl.pallas_call(functools.partial(project_kernel, chip_order, cap), in_spe...]
    ppermute x0 -> x30, starting transfers between devices: none -> 36.3 us  [the longest x19 18.3 us: swap(): return lax.ppermute(x, 'tensor', [(i, i ^ mask) for i in range(tensors)])]
    psum x2 -> x0, blocking collectives: 20.1 us -> none  [the longest x1 11.7 us: row_backward(): squares = lax.psum(jnp.sum(combined * combined, axis=1), 'group')]
    reduce_sum x6 -> x0, other arithmetic: 3.38 us -> none  [the longest x1 1.34 us: row_backward(): inner = lax.psum(jnp.sum(gain[None, :] * slope * combined, axis=1), 'group')]
  transfers between devices with their start and end apart: 4 -> 30, of which waited for: 4 -> 16; matrix products, arithmetic and copies ran while one was open for 2% -> 4% of each run, Pallas kernels for 0% -> 10%
where the time goes in v1:
time: 173 us
  waiting for transfers between devices  86 us (50%)
  Pallas kernels  41.4 us (24%)
  starting transfers between devices  36.3 us (21%)
  other arithmetic  6.4 us (4%)
    ppermute x11, waiting for transfers between devices, cross(): return lax.ppermute(x, 'group', [(i, i ^ mask) for i in range(groups)])  48.3 us
    ppermute x19, waiting for transfers between devices, swap(): return lax.ppermute(x, 'tensor', [(i, i ^ mask) for i in range(tensors)])  37.7 us
    ppermute x19, starting transfers between devices, swap(): return lax.ppermute(x, 'tensor', [(i, i ^ mask) for i in range(tensors)])  18.3 us
    ppermute x11, starting transfers between devices, cross(): return lax.ppermute(x, 'group', [(i, i ^ mask) for i in range(groups)])  18.1 us
    pallas_call x1, Pallas kernels, project(): pl.pallas_call(functools.partial(project_kernel, chip_order, cap), in_spe...  15.2 us
    pallas_call x1, Pallas kernels, finish(): pl.pallas_call(kernel, in_specs=[VMEM] * (7 + len(arrays)), out_specs=[VM...  9.85 us
    pallas_call x2, Pallas kernels, join_call(): pl.pallas_call(kernel, in_specs=[SMEM] + [VMEM] * (len(operands) - 1) + [...  8.5 us
    convert_element_type x2, other arithmetic, shards(): sent = value(going).astype(bf16)  3.61 us
  transfers between devices with their start and end apart: 30, of which 16 were waited for; matrix products, arithmetic and copies ran while one was open for 4% of the time, Pallas kernels for 10%

profile of v1, /device:TPU:0, one launch (start us, length us, event | category | flops | bytes accessed | tf_op | source)
XLA Modules:
  0.0 172.6 jit_solution(8262039816621655946)
XLA Ops:
  0.6 15.2 %project.1 = (bf16[4,128,1024]{2,1,0:T(8,128)(2,1)}, bf16[4,128,1024]{2,1,0:T(8,128)(2,1)S(1)}, bf16[128,1024]{1,0:T(8,128)(2,1)S(1)}, bf16[4,384,1024]{2,1,0:T(...) custom-call(s32[4,512]{1,0:T(4,128)} %rows_ref.5, bf16[512,1024]{1,0:T(8,128)(2,1)} %att_ref.1, ...), custom_call_target="tpu_custom_call" | custom-call | flops 8589934592 | bytes 25165824 | tf_op jit(solution)/shard_map/project/pallas_call | solution.py:179
  16.4 2.6 %early_rows.1 = (bf16[2,128,1024]{2,1,0:T(8,128)(2,1)S(1)}, bf16[2,64,1024]{2,1,0:T(8,128)(2,1)}) custom-call(s32[4,512]{1,0:T(4,128)} %rows_ref.5, bf16[512,1024]{1,0:T(8,128)(2,1)} %low_ref.1, bf16[512,1024]{1,0:T(8,128)(2,1)} %mid_ref.1), custom_call_target="tpu_custom_call" | custom-call | flops 268435456 | bytes 2621440 | tf_op jit(solution)/shard_map/early_rows/pallas_call | solution.py:79
  19.0 2.7 %collective-permute-start.9 = (bf16[2,128,1024]{2,1,0:T(8,128)(2,1)S(1)}, bf16[2,128,1024]{2,1,0:T(8,128)(2,1)S(1)}, u32[]{:S(2)}, u32[]{:S(2)}) collective-permute-start(bf16[2,128,1024]{2,1,0:T(8,128)(2,1)S(1)} %get-tuple-element.39.refs_0_), channel_id=1, source_target_pairs={{0,8},{8,0},{16,24},{24,16},{1,9},{9,1},{17,25},{25,17},{2,10},{10... | collective-permute-start | bytes 1572872 | tf_op jit(solution)/shard_map/ppermute | solution.py:613
  27.2 7.0 %collective-permute-done.9.refs_1_ = bf16[2,128,1024]{2,1,0:T(8,128)(2,1)S(1)} collective-permute-done((bf16[2,128,1024]{2,1,0:T(8,128)(2,1)S(1)}, bf16[2,128,1024]{2,1,0:T(8,128)(2,1)S(1)}, u32[]{:S(2)}, u32[]{:S(2)}) %collective-permute-start.9) | collective-permute-done | bytes 524320 | tf_op jit(solution)/shard_map/ppermute | solution.py:613
  34.2 2.8 %collective-permute-start.12 = (bf16[2,64,1024]{2,1,0:T(8,128)(2,1)S(1)}, bf16[2,64,1024]{2,1,0:T(8,128)(2,1)S(1)}, u32[]{:S(2)}, u32[]{:S(2)}) collective-permute-start(bf16[2,64,1024]{2,1,0:T(8,128)(2,1)S(1)} %slice_select_fusion), channel_id=1, source_target_pairs={{0,16},{8,24},{16,0},{24,8},{1,17},{9,25},{17,1},{25,9},{2,18},{10... | collective-permute-start | bytes 786440 | tf_op jit(solution)/shard_map/ppermute | solution.py:613
  37.0 1.8 %collective-permute-done.2.refs_1_ = bf16[128,1024]{1,0:T(8,128)(2,1)S(1)} collective-permute-done((bf16[128,1024]{1,0:T(8,128)(2,1)S(1)}, bf16[128,1024]{1,0:T(8,128)(2,1)S(1)}, u32[]{:S(2)}, u32[]{:S(2)}) %collective-permute-start.2) | collective-permute-done | bytes 262176 | tf_op jit(solution)/shard_map/ppermute | solution.py:610
  40.9 3.6 %collective-permute-start.11 = (bf16[2,64,1024]{2,1,0:T(8,128)(2,1)}, bf16[2,64,1024]{2,1,0:T(8,128)(2,1)S(1)}, u32[]{:S(2)}, u32[]{:S(2)}) collective-permute-start(bf16[2,64,1024]{2,1,0:T(8,128)(2,1)} %get-tuple-element.40), channel_id=1, source_target_pairs={{0,24},{8,16},{16,8},{24,0},{1,25},{9,17},{17,9},{25,1},{2,26},{10... | collective-permute-start | bytes 786440 | tf_op jit(solution)/shard_map/ppermute | solution.py:613
  44.5 7.3 %collective-permute-done.12 = bf16[2,64,1024]{2,1,0:T(8,128)(2,1)S(1)} collective-permute-done((bf16[2,64,1024]{2,1,0:T(8,128)(2,1)S(1)}, bf16[2,64,1024]{2,1,0:T(8,128)(2,1)S(1)}, u32[]{:S(2)}, u32[]{:S(2)}) %collective-permute-start.12) | collective-permute-done | bytes 262176 | tf_op jit(solution)/shard_map/ppermute | solution.py:613
  51.8 6.0 %collective-permute-done.13.refs_1_ = bf16[1,128,1024]{2,1,0:T(8,128)(2,1)S(1)} collective-permute-done((bf16[1,128,1024]{2,1,0:T(8,128)(2,1)S(1)}, bf16[1,128,1024]{2,1,0:T(8,128)(2,1)S(1)}, u32[]{:S(2)}, u32[]{:S(2)}) %collective-permute-start.13) | collective-permute-done | bytes 262176 | tf_op jit(solution)/shard_map/ppermute | solution.py:613
  59.3 15.9 %collective-permute-done.10.refs_2_ = bf16[2,64,1024]{2,1,0:T(8,128)(2,1)S(1)} collective-permute-done((bf16[2,64,1024]{2,1,0:T(8,128)(2,1)}, bf16[2,64,1024]{2,1,0:T(8,128)(2,1)S(1)}, u32[]{:S(2)}, u32[]{:S(2)}) %collective-permute-start.10) | collective-permute-done | bytes 262176 | tf_op jit(solution)/shard_map/ppermute | solution.py:613
  75.2 6.4 %join_early.1 = (bf16[2,256,1024]{2,1,0:T(8,128)(2,1)S(1)}, f32[256,2048]{1,0:T(8,128)S(1)}, bf16[1024,2048]{1,0:T(8,128)(2,1)S(1)}) custom-call(s32[4]{0:T(128)S(1)} %copy-done.3, bf16[2,128,1024]{2,1,0:T(8,128)(2,1)S(1)} %get-tuple-element.39.refs_0_, bf16[2,128,1024]{2,1,0:T(8,128)(2,1)S(1)} %collective-permute-done.9.refs_1_, ...), custom_call_target="tpu_custom_call" | custom-call | flops 2147483648 | bytes 8388608 | tf_op jit(solution)/shard_map/join_early/pallas_call | solution.py:358
  81.6 2.6 %collective-permute-start.15 = (bf16[1,64,1024]{2,1,0:T(8,128)(2,1)S(1)}, bf16[1,64,1024]{2,1,0:T(8,128)(2,1)S(1)}, u32[]{:S(2)}, u32[]{:S(2)}) collective-permute-start(bf16[1,64,1024]{2,1,0:T(8,128)(2,1)S(1)} %get-tuple-element.43), channel_id=1, source_target_pairs={{0,24},{8,16},{16,8},{24,0},{1,25},{9,17},{17,9},{25,1},{2,26},{10... | collective-permute-start | bytes 393224 | tf_op jit(solution)/shard_map/ppermute | solution.py:613
  84.2 5.1 %collective-permute-done.15.refs_3_ = bf16[1,64,1024]{2,1,0:T(8,128)(2,1)S(1)} collective-permute-done((bf16[1,64,1024]{2,1,0:T(8,128)(2,1)S(1)}, bf16[1,64,1024]{2,1,0:T(8,128)(2,1)S(1)}, u32[]{:S(2)}, u32[]{:S(2)}) %collective-permute-start.15) | collective-permute-done | bytes 131104 | tf_op jit(solution)/shard_map/ppermute | solution.py:613
  89.3 5.4 %collective-permute-done.14.refs_2_ = bf16[1,64,1024]{2,1,0:T(8,128)(2,1)S(1)} collective-permute-done((bf16[1,64,1024]{2,1,0:T(8,128)(2,1)S(1)}, bf16[1,64,1024]{2,1,0:T(8,128)(2,1)S(1)}, u32[]{:S(2)}, u32[]{:S(2)}) %collective-permute-start.14) | collective-permute-done | bytes 131104 | tf_op jit(solution)/shard_map/ppermute | solution.py:613
  94.7 2.1 %join_late.1 = (bf16[1,256,1024]{2,1,0:T(8,128)(2,1)S(1)}, f32[128,2048]{1,0:T(8,128)S(1)}, bf16[128,2048]{1,0:T(8,128)(2,1)S(1)}) custom-call(s32[4]{0:T(128)S(1)} %copy-done.3, bf16[1,128,1024]{2,1,0:T(8,128)(2,1)S(1)} %get-tuple-element.35.refs_0_, bf16[1,128,1024]{2,1,0:T(8,128)(2,1)S(1)} %collective-permute-done.13.refs_1_, ...), custom_call_target="tpu_custom_call" | custom-call | flops 1073741824 | bytes 4194304 | tf_op jit(solution)/shard_map/join_late/pallas_call | solution.py:358
  100.6 1.6 collective-permute-start.19
  103.7 2.1 %add_convert_fusion = (bf16[2,192,1024]{2,1,0:T(8,128)(2,1)S(1)}, bf16[2,192,1024]{2,1,0:T(8,128)(2,1)S(1)}) fusion(bf16[4,384,1024]{2,1,0:T(8,128)(2,1)} %collective-permute-done.4, bf16[4,384,1024]{2,1,0:T(8,128)(2,1)S(1)} %copy-done.4), kind=kLoop, calls=%fused_computation.2 | loop fusion | flops 3145728 | bytes 4718592 | tf_op jit(solution)/shard_map/convert_element_type | solution.py:672
  109.3 3.9 %collective-permute-done.24.refs_3_ = bf16[64,2048]{1,0:T(8,128)(2,1)S(1)} collective-permute-done((bf16[64,2048]{1,0:T(8,128)(2,1)S(1)}, bf16[64,2048]{1,0:T(8,128)(2,1)S(1)}, u32[]{:S(2)}, u32[]{:S(2)}) %collective-permute-start.24) | collective-permute-done | bytes 262176 | tf_op jit(solution)/shard_map/ppermute | solution.py:610
  114.0 3.4 %goals.1 = (bf16[128,2048]{1,0:T(8,128)(2,1)S(1)}, bf16[128,2048]{1,0:T(8,128)(2,1)S(1)}) custom-call(s32[4]{0:T(128)S(1)} %copy-done.3, s32[4,512]{1,0:T(4,128)S(1)} %copy-done.1, bf16[64,2048]{1,0:T(8,128)(2,1)} %refs_0_.1, bf16[64,2048]{1,0:T(8,128)(2,1)} %copy-done.8, bf16[64,2048]{1,0:T(8,128)(2,1)} %copy-done.7, bf16[64,2048]{1,0:T(8,128)(2,1)} %copy-done.9), custom_call_target="tpu_custom_call" | custom-call | flops 268435456 | bytes 2097152 | tf_op jit(solution)/shard_map/goals/pallas_call | solution.py:420
  119.1 1.6 collective-permute-start.21
  121.2 19.4 %collective-permute-done.21.refs_3_ = bf16[128,1024]{1,0:T(8,128)(2,1)S(1)} collective-permute-done((bf16[128,1024]{1,0:T(8,128)(2,1)S(1)}, bf16[128,1024]{1,0:T(8,128)(2,1)S(1)}, u32[]{:S(2)}, u32[]{:S(2)}) %collective-permute-start.21) | collective-permute-done | bytes 262176 | tf_op jit(solution)/shard_map/ppermute | solution.py:610
  142.6 2.9 %collective-permute-start.26 = (f32[8,128]{1,0:T(8,128)S(1)}, f32[8,128]{1,0:T(8,128)S(1)}, u32[]{:S(2)}, u32[]{:S(2)}) collective-permute-start(f32[8,128]{1,0:T(8,128)S(1)} %get-tuple-element.53.refs_0_), channel_id=1, source_target_pairs={{0,8},{8,0},{16,24},{24,16},{1,9},{9,1},{17,25},{25,17},{2,10},{10... | collective-permute-start | bytes 12296 | tf_op jit(solution)/shard_map/ppermute | solution.py:613
  153.5 8.0 %collective-permute-done.8.refs_3_ = bf16[1,192,1024]{2,1,0:T(8,128)(2,1)S(1)} collective-permute-done((bf16[1,192,1024]{2,1,0:T(8,128)(2,1)S(1)}, bf16[1,192,1024]{2,1,0:T(8,128)(2,1)S(1)}, u32[]{:S(2)}, u32[]{:S(2)}) %collective-permute-start.8) | collective-permute-done | bytes 393248 | tf_op jit(solution)/shard_map/ppermute | solution.py:610
  162.6 9.8 %finish.1 = (bf16[512,1024]{1,0:T(8,128)(2,1)}, f32[3,1024,2048]{2,1,0:T(8,128)}) custom-call(s32[4,512]{1,0:T(4,128)S(1)} %copy-done.2, bf16[128,1024]{1,0:T(8,128)(2,1)S(1)} %bitcast.10, f32[384,1024]{1,0:T(8,128)S(1)} %convert_add_fusion.base_ref, bf16[2,192,1024]{2,1,0:T(8,128)(2,1)S(1)} %collective-permute-done.5.refs_0_, ...), custom_call_target="tpu_custom_call" | custom-call | flops 3221225472 | bytes 25165824 | tf_op jit(solution)/shard_map/finish/pallas_call | solution.py:561
  (77 shorter events, 32.0 us)
Async XLA Ops:
  15.8 7.5 %collective-permute-start = (bf16[4,128,1024]{2,1,0:T(8,128)(2,1)}, bf16[4,128,1024]{2,1,0:T(8,128)(2,1)S(1)}, u32[]{:S(2)}, u32[]{:S(2)}) collective-permute-start(bf16[4,128,1024]{2,1,0:T(8,128)(2,1)} %get-tuple-element.29), channel_id=1, source_target_pairs={{0,1},{1,0},{2,3},{3,2},{4,5},{5,4},{6,7},{7,6},{8,9},{9,8},{10,11... | collective-permute-start | bytes 3145736 | tf_op jit(solution)/shard_map/ppermute | solution.py:610
  19.0 15.2 %collective-permute-start.9 = (bf16[2,128,1024]{2,1,0:T(8,128)(2,1)S(1)}, bf16[2,128,1024]{2,1,0:T(8,128)(2,1)S(1)}, u32[]{:S(2)}, u32[]{:S(2)}) collective-permute-start(bf16[2,128,1024]{2,1,0:T(8,128)(2,1)S(1)} %get-tuple-element.39.refs_0_), channel_id=1, source_target_pairs={{0,8},{8,0},{16,24},{24,16},{1,9},{9,1},{17,25},{25,17},{2,10},{10... | collective-permute-start | bytes 1572872 | tf_op jit(solution)/shard_map/ppermute | solution.py:613
  21.6 80.6 %collective-permute-start.4 = (bf16[4,384,1024]{2,1,0:T(8,128)(2,1)}, bf16[4,384,1024]{2,1,0:T(8,128)(2,1)}, u32[]{:S(2)}, u32[]{:S(2)}) collective-permute-start(bf16[4,384,1024]{2,1,0:T(8,128)(2,1)} %get-tuple-element.38), channel_id=1, source_target_pairs={{0,1},{1,0},{2,3},{3,2},{4,5},{5,4},{6,7},{7,6},{8,9},{9,8},{10,11... | collective-permute-start | bytes 9437192 | tf_op jit(solution)/shard_map/ppermute | solution.py:610
  23.6 13.4 %collective-permute-start.1 = (bf16[128,1024]{1,0:T(8,128)(2,1)S(1)}, bf16[128,1024]{1,0:T(8,128)(2,1)S(1)}, u32[]{:S(2)}, u32[]{:S(2)}) collective-permute-start(bf16[128,1024]{1,0:T(8,128)(2,1)S(1)} %get-tuple-element.32), channel_id=1, source_target_pairs={{0,2},{1,3},{2,0},{3,1},{4,6},{5,7},{6,4},{7,5},{8,10},{9,11},{10,... | collective-permute-start | bytes 786440 | tf_op jit(solution)/shard_map/ppermute | solution.py:610
  25.2 13.7 %collective-permute-start.2 = (bf16[128,1024]{1,0:T(8,128)(2,1)S(1)}, bf16[128,1024]{1,0:T(8,128)(2,1)S(1)}, u32[]{:S(2)}, u32[]{:S(2)}) collective-permute-start(bf16[128,1024]{1,0:T(8,128)(2,1)S(1)} %get-tuple-element.33), channel_id=1, source_target_pairs={{0,6},{1,7},{2,4},{3,5},{4,2},{5,3},{6,0},{7,1},{8,14},{9,15},{10,... | collective-permute-start | bytes 786440 | tf_op jit(solution)/shard_map/ppermute | solution.py:610
  26.7 13.6 %collective-permute-start.3 = (bf16[128,1024]{1,0:T(8,128)(2,1)S(1)}, bf16[128,1024]{1,0:T(8,128)(2,1)S(1)}, u32[]{:S(2)}, u32[]{:S(2)}) collective-permute-start(bf16[128,1024]{1,0:T(8,128)(2,1)S(1)} %get-tuple-element.34), channel_id=1, source_target_pairs={{0,4},{1,5},{2,6},{3,7},{4,0},{5,1},{6,2},{7,3},{8,12},{9,13},{10,... | collective-permute-start | bytes 786440 | tf_op jit(solution)/shard_map/ppermute | solution.py:610
  34.2 17.5 %collective-permute-start.12 = (bf16[2,64,1024]{2,1,0:T(8,128)(2,1)S(1)}, bf16[2,64,1024]{2,1,0:T(8,128)(2,1)S(1)}, u32[]{:S(2)}, u32[]{:S(2)}) collective-permute-start(bf16[2,64,1024]{2,1,0:T(8,128)(2,1)S(1)} %slice_select_fusion), channel_id=1, source_target_pairs={{0,16},{8,24},{16,0},{24,8},{1,17},{9,25},{17,1},{25,9},{2,18},{10... | collective-permute-start | bytes 786440 | tf_op jit(solution)/shard_map/ppermute | solution.py:613
  40.4 17.4 %collective-permute-start.13 = (bf16[1,128,1024]{2,1,0:T(8,128)(2,1)S(1)}, bf16[1,128,1024]{2,1,0:T(8,128)(2,1)S(1)}, u32[]{:S(2)}, u32[]{:S(2)}) collective-permute-start(bf16[1,128,1024]{2,1,0:T(8,128)(2,1)S(1)} %get-tuple-element.35.refs_0_), channel_id=1, source_target_pairs={{0,8},{8,0},{16,24},{24,16},{1,9},{9,1},{17,25},{25,17},{2,10},{10... | collective-permute-start | bytes 786440 | tf_op jit(solution)/shard_map/ppermute | solution.py:613
  40.9 18.4 %collective-permute-start.11 = (bf16[2,64,1024]{2,1,0:T(8,128)(2,1)}, bf16[2,64,1024]{2,1,0:T(8,128)(2,1)S(1)}, u32[]{:S(2)}, u32[]{:S(2)}) collective-permute-start(bf16[2,64,1024]{2,1,0:T(8,128)(2,1)} %get-tuple-element.40), channel_id=1, source_target_pairs={{0,24},{8,16},{16,8},{24,0},{1,25},{9,17},{17,9},{25,1},{2,26},{10... | collective-permute-start | bytes 786440 | tf_op jit(solution)/shard_map/ppermute | solution.py:613
  44.5 30.8 %collective-permute-start.10 = (bf16[2,64,1024]{2,1,0:T(8,128)(2,1)}, bf16[2,64,1024]{2,1,0:T(8,128)(2,1)S(1)}, u32[]{:S(2)}, u32[]{:S(2)}) collective-permute-start(bf16[2,64,1024]{2,1,0:T(8,128)(2,1)} %get-tuple-element.40), channel_id=1, source_target_pairs={{0,16},{8,24},{16,0},{24,8},{1,17},{9,25},{17,1},{25,9},{2,18},{10... | collective-permute-start | bytes 786440 | tf_op jit(solution)/shard_map/ppermute | solution.py:613
  57.8 26.4 %collective-permute-start.16 = (bf16[1,64,1024]{2,1,0:T(8,128)(2,1)S(1)}, bf16[1,64,1024]{2,1,0:T(8,128)(2,1)S(1)}, u32[]{:S(2)}, u32[]{:S(2)}) collective-permute-start(bf16[1,64,1024]{2,1,0:T(8,128)(2,1)S(1)} %slice_select_fusion.1), channel_id=1, source_target_pairs={{0,16},{8,24},{16,0},{24,8},{1,17},{9,25},{17,1},{25,9},{2,18},{10... | collective-permute-start | bytes 393224 | tf_op jit(solution)/shard_map/ppermute | solution.py:613
  81.6 7.6 %collective-permute-start.15 = (bf16[1,64,1024]{2,1,0:T(8,128)(2,1)S(1)}, bf16[1,64,1024]{2,1,0:T(8,128)(2,1)S(1)}, u32[]{:S(2)}, u32[]{:S(2)}) collective-permute-start(bf16[1,64,1024]{2,1,0:T(8,128)(2,1)S(1)} %get-tuple-element.43), channel_id=1, source_target_pairs={{0,24},{8,16},{16,8},{24,0},{1,25},{9,17},{17,9},{25,1},{2,26},{10... | collective-permute-start | bytes 393224 | tf_op jit(solution)/shard_map/ppermute | solution.py:613
  84.2 10.5 %collective-permute-start.14 = (bf16[1,64,1024]{2,1,0:T(8,128)(2,1)S(1)}, bf16[1,64,1024]{2,1,0:T(8,128)(2,1)S(1)}, u32[]{:S(2)}, u32[]{:S(2)}) collective-permute-start(bf16[1,64,1024]{2,1,0:T(8,128)(2,1)S(1)} %get-tuple-element.43), channel_id=1, source_target_pairs={{0,16},{8,24},{16,0},{24,8},{1,17},{9,25},{17,1},{25,9},{2,18},{10... | collective-permute-start | bytes 393224 | tf_op jit(solution)/shard_map/ppermute | solution.py:613
  96.9 9.4 %collective-permute-start.23 = (bf16[64,2048]{1,0:T(8,128)(2,1)S(1)}, bf16[64,2048]{1,0:T(8,128)(2,1)S(1)}, u32[]{:S(2)}, u32[]{:S(2)}) collective-permute-start(bf16[64,2048]{1,0:T(8,128)(2,1)S(1)} %copy-done.6), channel_id=1, source_target_pairs={{0,4},{1,5},{2,6},{3,7},{4,0},{5,1},{6,2},{7,3},{8,12},{9,13},{10,... | collective-permute-start | bytes 786440 | tf_op jit(solution)/shard_map/ppermute | solution.py:610
  98.4 9.4 %collective-permute-start.22 = (bf16[64,2048]{1,0:T(8,128)(2,1)S(1)}, bf16[64,2048]{1,0:T(8,128)(2,1)S(1)}, u32[]{:S(2)}, u32[]{:S(2)}) collective-permute-start(bf16[64,2048]{1,0:T(8,128)(2,1)S(1)} %copy-done.6), channel_id=1, source_target_pairs={{0,2},{1,3},{2,0},{3,1},{4,6},{5,7},{6,4},{7,5},{8,10},{9,11},{10,... | collective-permute-start | bytes 786440 | tf_op jit(solution)/shard_map/ppermute | solution.py:610
  99.9 13.3 %collective-permute-start.24 = (bf16[64,2048]{1,0:T(8,128)(2,1)S(1)}, bf16[64,2048]{1,0:T(8,128)(2,1)S(1)}, u32[]{:S(2)}, u32[]{:S(2)}) collective-permute-start(bf16[64,2048]{1,0:T(8,128)(2,1)S(1)} %copy-done.6), channel_id=1, source_target_pairs={{0,6},{1,7},{2,4},{3,5},{4,2},{5,3},{6,0},{7,1},{8,14},{9,15},{10,... | collective-permute-start | bytes 786440 | tf_op jit(solution)/shard_map/ppermute | solution.py:610
  100.6 16.8 %collective-permute-start.19 = (bf16[128,1024]{1,0:T(8,128)(2,1)S(1)}, bf16[128,1024]{1,0:T(8,128)(2,1)S(1)}, u32[]{:S(2)}, u32[]{:S(2)}) collective-permute-start(bf16[128,1024]{1,0:T(8,128)(2,1)S(1)} %get-tuple-element.64), channel_id=1, source_target_pairs={{0,4},{1,5},{2,6},{3,7},{4,0},{5,1},{6,2},{7,3},{8,12},{9,13},{10,... | collective-permute-start | bytes 786440 | tf_op jit(solution)/shard_map/ppermute | solution.py:610
  102.2 16.7 %collective-permute-start.18 = (bf16[128,1024]{1,0:T(8,128)(2,1)S(1)}, bf16[128,1024]{1,0:T(8,128)(2,1)S(1)}, u32[]{:S(2)}, u32[]{:S(2)}) collective-permute-start(bf16[128,1024]{1,0:T(8,128)(2,1)S(1)} %get-tuple-element.65), channel_id=1, source_target_pairs={{0,2},{1,3},{2,0},{3,1},{4,6},{5,7},{6,4},{7,5},{8,10},{9,11},{10,... | collective-permute-start | bytes 786440 | tf_op jit(solution)/shard_map/ppermute | solution.py:610
  106.3 42.0 %collective-permute-start.7 = (bf16[2,192,1024]{2,1,0:T(8,128)(2,1)S(1)}, bf16[2,192,1024]{2,1,0:T(8,128)(2,1)S(1)}, u32[]{:S(2)}, u32[]{:S(2)}) collective-permute-start(bf16[2,192,1024]{2,1,0:T(8,128)(2,1)S(1)} %get-tuple-element.60), channel_id=1, source_target_pairs={{0,4},{1,5},{2,6},{3,7},{4,0},{5,1},{6,2},{7,3},{8,12},{9,13},{10,... | collective-permute-start | bytes 2359304 | tf_op jit(solution)/shard_map/ppermute | solution.py:610
  107.8 40.5 %collective-permute-start.5 = (bf16[2,192,1024]{2,1,0:T(8,128)(2,1)S(1)}, bf16[2,192,1024]{2,1,0:T(8,128)(2,1)S(1)}, u32[]{:S(2)}, u32[]{:S(2)}) collective-permute-start(bf16[2,192,1024]{2,1,0:T(8,128)(2,1)S(1)} %get-tuple-element.61), channel_id=1, source_target_pairs={{0,2},{1,3},{2,0},{3,1},{4,6},{5,7},{6,4},{7,5},{8,10},{9,11},{10,... | collective-permute-start | bytes 2359304 | tf_op jit(solution)/shard_map/ppermute | solution.py:610
  119.1 21.5 %collective-permute-start.21 = (bf16[128,1024]{1,0:T(8,128)(2,1)S(1)}, bf16[128,1024]{1,0:T(8,128)(2,1)S(1)}, u32[]{:S(2)}, u32[]{:S(2)}) collective-permute-start(bf16[128,1024]{1,0:T(8,128)(2,1)S(1)} %get-tuple-element.54), channel_id=1, source_target_pairs={{0,2},{1,3},{2,0},{3,1},{4,6},{5,7},{6,4},{7,5},{8,10},{9,11},{10,... | collective-permute-start | bytes 786440 | tf_op jit(solution)/shard_map/ppermute | solution.py:610
  120.6 19.9 %collective-permute-start.20 = (bf16[128,1024]{1,0:T(8,128)(2,1)S(1)}, bf16[128,1024]{1,0:T(8,128)(2,1)S(1)}, u32[]{:S(2)}, u32[]{:S(2)}) collective-permute-start(bf16[128,1024]{1,0:T(8,128)(2,1)S(1)} %get-tuple-element.62), channel_id=1, source_target_pairs={{0,4},{1,5},{2,6},{3,7},{4,0},{5,1},{6,2},{7,3},{8,12},{9,13},{10,... | collective-permute-start | bytes 786440 | tf_op jit(solution)/shard_map/ppermute | solution.py:610
  149.8 11.6 %collective-permute-start.8 = (bf16[1,192,1024]{2,1,0:T(8,128)(2,1)S(1)}, bf16[1,192,1024]{2,1,0:T(8,128)(2,1)S(1)}, u32[]{:S(2)}, u32[]{:S(2)}) collective-permute-start(bf16[1,192,1024]{2,1,0:T(8,128)(2,1)S(1)} %get-tuple-element.58), channel_id=1, source_target_pairs={{0,2},{1,3},{2,0},{3,1},{4,6},{5,7},{6,4},{7,5},{8,10},{9,11},{10,... | collective-permute-start | bytes 1179656 | tf_op jit(solution)/shard_map/ppermute | solution.py:610
  151.4 11.2 %collective-permute-start.6 = (bf16[1,192,1024]{2,1,0:T(8,128)(2,1)S(1)}, bf16[1,192,1024]{2,1,0:T(8,128)(2,1)S(1)}, u32[]{:S(2)}, u32[]{:S(2)}) collective-permute-start(bf16[1,192,1024]{2,1,0:T(8,128)(2,1)S(1)} %get-tuple-element.59), channel_id=1, source_target_pairs={{0,4},{1,5},{2,6},{3,7},{4,0},{5,1},{6,2},{7,3},{8,12},{9,13},{10,... | collective-permute-start | bytes 1179656 | tf_op jit(solution)/shard_map/ppermute | solution.py:610
  (16 other events, 144.1 us)

commit v2 on v1

--- a/solution.py
+++ b/solution.py
@@ -92,158 +92,198 @@
     )(*in_hbm(accept_rows, low, mid))
 
 
+def weight_blocks(order, w_ref, weights, sem):
+    t = lax.axis_index("tensor")
+    width = weights.shape[2]
+    copies = []
+    for i, block in enumerate(order):
+        at = pl.ds(pl.multiple_of((t ^ block) * width, 128), width)
+        copies.append(pltpu.make_async_copy(w_ref.at[:, at], weights.at[i], sem.at[i]))
+    return copies
+
+
+ahead = 3
+
+
 def project_kernel(
     chip_order,
-    cap,
     rows_ref,
     att_ref,
     res_ref,
     w_ref,
-    give_acc,
-    keep_acc,
-    res_acc,
-    give_rest,
-    keep_rest,
+    give,
+    keep,
     res_rest,
+    x_rest,
     ids,
     att,
     res,
+    sent,
     picked,
-    wbuf,
-    obuf,
+    weights,
     sem,
+    put_sem,
     small_sem,
 ):
     chips = len(chip_order)
-    width = wbuf.shape[2]
-    rows = att.shape[0]
-    t = lax.axis_index("tensor")
-
-    def fetch(i, block):
-        at = pl.ds(pl.multiple_of((t ^ block) * width, 128), width)
-        return pltpu.make_async_copy(w_ref.at[:, at], wbuf.at[i], sem.at[0, i])
+    cap = keep.shape[1]
+    order = [2 * m + 1 for m in chip_order] + [2 * m for m in chip_order]
+    fetch = weight_blocks(order, w_ref, weights, sem)
 
     def put(i):
-        j = i % chips
-        rest = give_rest if i < chips else keep_rest
-        copies = [
-            pltpu.make_async_copy(
-                obuf.at[i, pl.ds(cap, rows - cap)], rest.at[j], sem.at[1, i]
-            )
-        ]
+        return pltpu.make_async_copy(sent.at[i], give.at[i], put_sem.at[i])
+
+    copies = fetch_all([(rows_ref, ids), (att_ref, att), (res_ref, res)], small_sem)
+    for copy in fetch[:ahead]:
+        copy.start()
+    copies[0].wait()
+    place = place_of(ids, 0, att.shape[0], lax.axis_index("group"))
+    copies[1].wait()
+    x = pick_rows(place[:, :cap], att[...])
+    puts = [
+        pltpu.make_async_copy(picked.at[0], x_rest, small_sem.at[3]),
+        pltpu.make_async_copy(picked.at[1], res_rest, small_sem.at[4]),
+    ]
+    for i, copy in enumerate(fetch):
+        if i == 1:
+            picked[0] = pick_rows(place[:, cap:], att[...])
+            puts[0].start()
+        if i == 2:
+            copies[2].wait()
+            keep[chips] = pick_rows(place[:, :cap], res[...])
+        if i == 3:
+            picked[1] = pick_rows(place[:, cap:], res[...])
+            puts[1].start()
+        copy.wait()
+        if i + ahead < len(fetch):
+            fetch[i + ahead].start()
+        y = jnp.dot(x, weights[i], preferred_element_type=f32).astype(bf16)
         if i < chips:
-            copies.append(
-                pltpu.make_async_copy(
-                    obuf.at[i, pl.ds(0, cap)], give_acc.at[j], sem.at[2, i]
-                )
-            )
-        return copies
-
-    order = [2 * m + 1 for m in chip_order] + [2 * m for m in chip_order]
-    ahead = 3
-    copies = fetch_all([(rows_ref, ids), (att_ref, att)], small_sem)
-    late = pltpu.make_async_copy(res_ref, res, small_sem.at[2])
-    for i in range(ahead):
-        fetch(i, order[i]).start()
-    copies[0].wait()
-    place = place_of(ids, 0, rows, lax.axis_index("group"))
-    copies[1].wait()
-    x = pick_rows(place, att[...])
-    for i, block in enumerate(order):
-        fetch(i, block).wait()
-        if i + ahead < len(order):
-            fetch(i + ahead, order[i + ahead]).start()
-        elif i + ahead == len(order):
-            late.start()
-        y = jnp.dot(x, wbuf[i], preferred_element_type=f32).astype(bf16)
-        obuf[i] = y
-        if i >= chips:
-            keep_acc[i - chips] = y[:cap]
-        for copy in put(i):
-            copy.start()
-    late.wait()
-    picked[...] = pick_rows(place, res[...])
-    res_acc[...] = picked[:cap]
-    last = pltpu.make_async_copy(picked.at[pl.ds(cap, rows - cap)], res_rest, small_sem.at[3])
-    last.start()
-    for i in range(2 * chips):
-        for copy in put(i):
-            copy.wait()
-    last.wait()
+            sent[i] = y
+            put(i).start()
+        else:
+            keep[i - chips] = y
+    for i in range(chips):
+        put(i).wait()
+    for copy in puts:
+        copy.wait()
 
 
 def project(accept_rows, attention, residual, o_weight, chip_order, cap, width):
     rows, depth = attention.shape
     chips = len(chip_order)
-    acc, rest = (chips, cap, width), (chips, rows - cap, width)
-    return pl.pallas_call(
-        functools.partial(project_kernel, chip_order, cap),
+    return pl.pallas_call(
+        functools.partial(project_kernel, chip_order),
         in_specs=[HBM] * 4,
-        out_specs=[HBM, VMEM, VMEM, HBM, HBM, HBM],
+        out_specs=[HBM, VMEM, HBM, HBM],
         out_shape=[
-            pltpu.HBM(acc, bf16),
-            jax.ShapeDtypeStruct(acc, bf16),
-            jax.ShapeDtypeStruct(acc[1:], bf16),
-            pltpu.HBM(rest, bf16),
-            pltpu.HBM(rest, bf16),
-            pltpu.HBM(rest[1:], bf16),
+            pltpu.HBM((chips, cap, width), bf16),
+            jax.ShapeDtypeStruct((chips + 1, cap, width), bf16),
+            pltpu.HBM((rows - cap, width), bf16),
+            pltpu.HBM((rows - cap, depth), bf16),
         ],
         scratch_shapes=[
             pltpu.VMEM(accept_rows.shape, i32),
             pltpu.VMEM(attention.shape, bf16),
             pltpu.VMEM(residual.shape, bf16),
-            pltpu.VMEM(residual.shape, bf16),
+            pltpu.VMEM((chips, cap, width), bf16),
+            pltpu.VMEM((2, rows - cap, width), bf16),
             pltpu.VMEM((2 * chips, depth, width), bf16),
-            pltpu.VMEM((2 * chips, rows, width), bf16),
-            pltpu.SemaphoreType.DMA((3, 2 * chips)),
-            pltpu.SemaphoreType.DMA((4,)),
+            pltpu.SemaphoreType.DMA((2 * chips,)),
+            pltpu.SemaphoreType.DMA((chips,)),
+            pltpu.SemaphoreType.DMA((5,)),
         ],
-        compiler_params=params(36),
-        cost_estimate=cost(
-            4 * rows * depth * width * chips, 4 * depth * width * chips + 4 * rows * width * chips
-        ),
+        compiler_params=params(28),
+        cost_estimate=cost(4 * cap * depth * width * chips, 4 * depth * width * chips),
         name="project",
     )(*in_hbm(accept_rows, attention, residual, o_weight))
 
 
-def pair_sums(keep, got, res):
-    chips, rows, width = keep.shape
-
-    def kernel(keep_ref, got_ref, res_ref, own_out, *outs):
+def project_rest(x, o_weight, chip_order, width):
+    rows, depth = x.shape
+    chips = len(chip_order)
+    blocks = 2 * chips
+    order = [2 * m + 1 for m in chip_order] + [2 * m for m in chip_order]
+
+    def kernel(x_ref, w_ref, give, keep, held, sent, weights, sem, put_sem):
+        fetch = weight_blocks(order, w_ref, weights, sem)
+        puts = [
+            pltpu.make_async_copy(
+                sent.at[i], (give if i < chips else keep).at[i % chips], put_sem.at[i]
+            )
+            for i in range(blocks)
+        ]
+        first = pltpu.make_async_copy(x_ref, held, put_sem.at[blocks])
+        first.start()
+        for copy in fetch[:ahead]:
+            copy.start()
+        first.wait()
+        for i, copy in enumerate(fetch):
+            copy.wait()
+            if i + ahead < blocks:
+                fetch[i + ahead].start()
+            sent[i] = jnp.dot(held[...], weights[i], preferred_element_type=f32).astype(bf16)
+            puts[i].start()
+        for copy in puts:
+            copy.wait()
+
+    shape = pltpu.HBM((chips, rows, width), bf16)
+    return pl.pallas_call(
+        kernel,
+        in_specs=[HBM] * 2,
+        out_specs=[HBM] * 2,
+        out_shape=[shape, shape],
+        scratch_shapes=[
+            pltpu.VMEM((rows, depth), bf16),
+            pltpu.VMEM((blocks, rows, width), bf16),
+            pltpu.VMEM((blocks, depth, width), bf16),
+            pltpu.SemaphoreType.DMA((blocks,)),
+            pltpu.SemaphoreType.DMA((blocks + 1,)),
+        ],
+        compiler_params=params(28),
+        cost_estimate=cost(2 * rows * depth * width * blocks, 2 * depth * width * blocks),
+        name="project_rest",
+    )(*in_hbm(x, o_weight))
+
+
+def pair_sums(keep, got):
+    chips, rows, width = got.shape
+
+    def kernel(keep_ref, got_ref, own_out, *outs):
         own_out[...] = (
-            res_ref[...].astype(f32) + keep_ref[0].astype(f32) + got_ref[0].astype(f32)
+            keep_ref[chips].astype(f32) + keep_ref[0].astype(f32) + got_ref[0].astype(f32)
         )
         for i, out in enumerate(outs):
             out[...] = (keep_ref[i + 1].astype(f32) + got_ref[i + 1].astype(f32)).astype(bf16)
 
     return pl.pallas_call(
         kernel,
-        in_specs=[VMEM] * 3,
+        in_specs=[VMEM] * 2,
         out_specs=[VMEM] * chips,
         out_shape=[jax.ShapeDtypeStruct((rows, width), f32)]
         + [jax.ShapeDtypeStruct((rows, width), bf16)] * (chips - 1),
         compiler_params=params(8),
         cost_estimate=cost(chips * rows * width, 6 * chips * rows * width),
         name="pair_sums",
-    )(keep, got, res)
+    )(keep, got)
 
 
 def top_rows(own, came, first):
     rows, width = own.shape
-    shapes = [(1, rows, width)] + ([(1, first, width)] if rows > first else [])
+    spans = [(0, rows)] + ([(0, first), (first, rows)] if rows > first else [])
 
     def kernel(own_ref, *refs):
         total = own_ref[...]
         for ref in refs[: len(came)]:
             total = total + ref[...].astype(f32)
-        for out in refs[len(came) :]:
-            out[0] = total[: out.shape[1]].astype(bf16)
+        for (lo, hi), out in zip(spans, refs[len(came) :]):
+            out[0] = total[lo:hi].astype(bf16)
 
     return pl.pallas_call(
         kernel,
         in_specs=[VMEM] * (1 + len(came)),
-        out_specs=[VMEM] * len(shapes),
-        out_shape=[jax.ShapeDtypeStruct(s, bf16) for s in shapes],
+        out_specs=[VMEM] * len(spans),
+        out_shape=[jax.ShapeDtypeStruct((1, hi - lo, width), bf16) for lo, hi in spans],
         compiler_params=params(8),
         cost_estimate=cost(4 * rows * width, 12 * rows * width),
         name="top_rows",
@@ -286,7 +326,7 @@
 
     def kernel(counts_ref, *refs):
         refs = list(refs)
-        blocks = [refs.pop(0) for _ in range(groups + has_extra)]
+        blocks = [refs.pop(0) for _ in range(groups + 2 * has_extra)]
         so_far_ref = refs.pop(0) if final else None
         w_ref = refs.pop(0)
         rows_out = refs.pop(0)
@@ -321,7 +361,10 @@
             for back in range(groups):
                 joined[i, back * common : (back + 1) * common] = blocks[back][i, :common]
             if has_extra:
-                joined[i, groups * common :] = blocks[groups][i]
+                crossed = ((busiest_of(counts_ref) ^ g) & (groups // 2)) != 0
+                joined[i, groups * common :] = jnp.where(
+                    crossed, blocks[groups + 1][i], blocks[groups][i]
+                )
             x = jnp.dot(place, joined[i], preferred_element_type=f32).astype(bf16)
             rows_out[i] = x
             if not final:
@@ -352,7 +395,7 @@
         ]
     operands = [counts, *gathered]
     if has_extra:
-        operands.append(extra)
+        operands.extend(extra)
     if final:
         operands.append(so_far)
     return pl.pallas_call(
@@ -612,39 +655,44 @@
     def cross(x, mask):
         return lax.ppermute(x, "group", [(i, i ^ mask) for i in range(groups)])
 
-    busiest = jnp.argmax(counts).astype(i32)
-
-    def gather(full, first):
-        blocks = [full, cross(full, 1)]
+    def gather(full, first, extra):
+        blocks = [first if extra is not None else full]
+        blocks += [cross(blocks[0], 1)]
         blocks += [cross(first, mask) for mask in range(2, groups)]
         if cap == common:
             return blocks, None
-        extra = jnp.where(
-            ((busiest ^ g) & 1) != 0, blocks[1][:, common:], full[:, common:]
-        )
-        for bit in group_bits[1:]:
-            other = cross(extra, bit)
+        if extra is None:
+            other, extra = blocks[1][:, common:], full[:, common:]
+        else:
+            other = cross(extra, 1)
+        busiest = jnp.argmax(counts).astype(i32)
+        for bit, after in zip(group_bits, group_bits[1:]):
             extra = jnp.where(((busiest ^ g) & bit) != 0, other, extra)
-        return blocks, extra
+            other = cross(extra, after)
+        return blocks, (extra, other)
 
     early = early_rows(accept_rows, low_state, mid_state, common, cap)
-    early_all, early_extra = gather(early[0], early[-1])
+    early_all, early_extra = gather(early[0], early[-1], None)
 
     targets = [target] + [swap(target, 2 * m) for m in range(1, chips)]
 
     gray = [i ^ (i >> 1) for i in range(chips)]
     at = {m: i for i, m in enumerate(gray)}
-    give_acc, keep_acc, res_acc, give_rest, keep_rest, res_rest = project(
+    give_acc, keep_acc, res_rest, x_rest = project(
         accept_rows, attention, residual, o_weight, gray, cap, width
     )
+    give_rest, keep_rest = project_rest(x_rest, o_weight, gray, width)
     got_acc = swap(give_acc, 1)
     got_rest = swap(give_rest, 1)
 
-    own, *others = pair_sums(keep_acc, got_acc, res_acc)
+    own, *others = pair_sums(keep_acc, got_acc)
     came = [swap(others[i - 1], 2 * gray[i]) for i in range(1, chips)]
     late = top_rows(own, came, common)
     top_acc = late[0][0]
-    late_all, late_extra = gather(late[0], late[-1])
+    if cap > common:
+        late_all, late_extra = gather(*late)
+    else:
+        late_all, late_extra = gather(late[0], late[0], None)
 
     n_rest = rows - cap
     base = res_rest.astype(f32) + keep_rest[0].astype(f32) + got_rest[0].astype(f32)

time: 173 us -> 166 us (0.960)
  waiting for transfers between devices: 86 us -> 65.1 us
  starting transfers between devices: 36.3 us -> 47.1 us
  Pallas kernels: 41.4 us -> 44.6 us
    ppermute x11 -> x12, waiting for transfers between devices: 48.3 us -> 23.6 us  [cross(): return lax.ppermute(x, 'group', [(i, i ^ mask) for i in range(groups)])]
    ppermute x11 -> x12, starting transfers between devices: 18.1 us -> 28.9 us  [cross(): return lax.ppermute(x, 'group', [(i, i ^ mask) for i in range(groups)])]
    pallas_call x2 -> x3, Pallas kernels: 15.4 us -> 19.2 us  [the longest x1 10.7 us: project_rest(): pl.pallas_call(kernel, in_specs=[HBM] * 2, out_specs=[HBM] * 2, out_shape...]
    ppermute x19, waiting for transfers between devices: 37.7 us -> 41.5 us  [swap(): return lax.ppermute(x, 'tensor', [(i, i ^ mask) for i in range(tensors)])]
  transfers between devices with their start and end apart: 30 -> 31, of which waited for: 16 -> 16; matrix products, arithmetic and copies ran while one was open for 4% -> 4% of each run, Pallas kernels for 10% -> 16%
where the time goes in v2:
time: 166 us
  waiting for transfers between devices  65.1 us (39%)
  starting transfers between devices  47.1 us (28%)
  Pallas kernels  44.6 us (27%)
  other arithmetic  6.44 us (4%)
  between operations  1.72 us (1%)
    ppermute x19, waiting for transfers between devices, swap(): return lax.ppermute(x, 'tensor', [(i, i ^ mask) for i in range(tensors)])  41.5 us
    ppermute x12, starting transfers between devices, cross(): return lax.ppermute(x, 'group', [(i, i ^ mask) for i in range(groups)])  28.9 us
    ppermute x12, waiting for transfers between devices, cross(): return lax.ppermute(x, 'group', [(i, i ^ mask) for i in range(groups)])  23.6 us
    ppermute x19, starting transfers between devices, swap(): return lax.ppermute(x, 'tensor', [(i, i ^ mask) for i in range(tensors)])  18.2 us
    pallas_call x1, Pallas kernels, project_rest(): pl.pallas_call(kernel, in_specs=[HBM] * 2, out_specs=[HBM] * 2, out_shape...  10.7 us
    pallas_call x1, Pallas kernels, finish(): pl.pallas_call(kernel, in_specs=[VMEM] * (7 + len(arrays)), out_specs=[VM...  9.84 us
    pallas_call x2, Pallas kernels, join_call(): pl.pallas_call(kernel, in_specs=[SMEM] + [VMEM] * (len(operands) - 1) + [...  8.49 us
    pallas_call x1, Pallas kernels, project(): pl.pallas_call(functools.partial(project_kernel, chip_order), in_specs=[H...  8.24 us
  transfers between devices with their start and end apart: 31, of which 16 were waited for; matrix products, arithmetic and copies ran while one was open for 4% of the time, Pallas kernels for 16%

profile of v2, /device:TPU:0, one launch (start us, length us, event | category | flops | bytes accessed | tf_op | source)
XLA Modules:
  0.0 165.8 jit_solution(3561042470245217253)
XLA Ops:
  0.6 8.2 %project.1 = (bf16[4,128,1024]{2,1,0:T(8,128)(2,1)}, bf16[5,128,1024]{2,1,0:T(8,128)(2,1)S(1)}, bf16[384,1024]{1,0:T(8,128)(2,1)}, bf16[384,1024]{1,0:T(8,128)(2,1)}) custom-call(s32[4,512]{1,0:T(4,128)} %rows_ref.5, bf16[512,1024]{1,0:T(8,128)(2,1)} %att_ref.1, bf16[512,1024]{1,0:T(8,128)(2,1)} %res_ref.1, bf16[1024,8192]{1,0:T(8,128)(2,1)} %w_ref.3), custom_call_target="tpu_custom_call" | custom-call | flops 2147483648 | bytes 16777216 | tf_op jit(solution)/shard_map/project/pallas_call | solution.py:175
  9.4 10.7 %project_rest.1 = (bf16[4,384,1024]{2,1,0:T(8,128)(2,1)}, bf16[4,384,1024]{2,1,0:T(8,128)(2,1)}) custom-call(bf16[384,1024]{1,0:T(8,128)(2,1)} %get-tuple-element.37.x_ref, bf16[1024,8192]{1,0:T(8,128)(2,1)} %w_ref.3), custom_call_target="tpu_custom_call" | custom-call | flops 6442450944 | bytes 16777216 | tf_op jit(solution)/shard_map/project_rest/pallas_call | solution.py:231
  20.3 1.9 %early_rows.1 = (bf16[2,128,1024]{2,1,0:T(8,128)(2,1)S(1)}, bf16[2,64,1024]{2,1,0:T(8,128)(2,1)S(1)}) custom-call(s32[4,512]{1,0:T(4,128)} %rows_ref.5, bf16[512,1024]{1,0:T(8,128)(2,1)} %low_ref.1, bf16[512,1024]{1,0:T(8,128)(2,1)} %mid_ref.1), custom_call_target="tpu_custom_call" | custom-call | flops 268435456 | bytes 2621440 | tf_op jit(solution)/shard_map/early_rows/pallas_call | solution.py:79
  22.2 3.1 %collective-permute-start.9 = (bf16[2,128,1024]{2,1,0:T(8,128)(2,1)S(1)}, bf16[2,128,1024]{2,1,0:T(8,128)(2,1)S(1)}, u32[]{:S(2)}, u32[]{:S(2)}) collective-permute-start(bf16[2,128,1024]{2,1,0:T(8,128)(2,1)S(1)} %get-tuple-element.40.refs_0_), channel_id=1, source_target_pairs={{0,8},{8,0},{16,24},{24,16},{1,9},{9,1},{17,25},{25,17},{2,10},{10... | collective-permute-start | bytes 1572872 | tf_op jit(solution)/shard_map/ppermute | solution.py:656
  30.7 4.1 %collective-permute-done.1.refs_0_ = bf16[128,1024]{1,0:T(8,128)(2,1)S(1)} collective-permute-done((bf16[128,1024]{1,0:T(8,128)(2,1)S(1)}, bf16[128,1024]{1,0:T(8,128)(2,1)S(1)}, u32[]{:S(2)}, u32[]{:S(2)}) %collective-permute-start.1) | collective-permute-done | bytes 262176 | tf_op jit(solution)/shard_map/ppermute | solution.py:653
  34.8 2.5 %collective-permute-start.11 = (bf16[2,64,1024]{2,1,0:T(8,128)(2,1)S(1)}, bf16[2,64,1024]{2,1,0:T(8,128)(2,1)S(1)}, u32[]{:S(2)}, u32[]{:S(2)}) collective-permute-start(bf16[2,64,1024]{2,1,0:T(8,128)(2,1)S(1)} %get-tuple-element.41), channel_id=1, source_target_pairs={{0,24},{8,16},{16,8},{24,0},{1,25},{9,17},{17,9},{25,1},{2,26},{10... | collective-permute-start | bytes 786440 | tf_op jit(solution)/shard_map/ppermute | solution.py:656
  37.3 3.0 %collective-permute-done.2.refs_1_ = bf16[128,1024]{1,0:T(8,128)(2,1)S(1)} collective-permute-done((bf16[128,1024]{1,0:T(8,128)(2,1)S(1)}, bf16[128,1024]{1,0:T(8,128)(2,1)S(1)}, u32[]{:S(2)}, u32[]{:S(2)}) %collective-permute-start.2) | collective-permute-done | bytes 262176 | tf_op jit(solution)/shard_map/ppermute | solution.py:653
  40.3 2.6 %collective-permute-start.10 = (bf16[2,64,1024]{2,1,0:T(8,128)(2,1)S(1)}, bf16[2,64,1024]{2,1,0:T(8,128)(2,1)S(1)}, u32[]{:S(2)}, u32[]{:S(2)}) collective-permute-start(bf16[2,64,1024]{2,1,0:T(8,128)(2,1)S(1)} %get-tuple-element.41), channel_id=1, source_target_pairs={{0,16},{8,24},{16,0},{24,8},{1,17},{9,25},{17,1},{25,9},{2,18},{10... | collective-permute-start | bytes 786440 | tf_op jit(solution)/shard_map/ppermute | solution.py:656
  45.0 7.4 %collective-permute-done.16 = bf16[1,64,1024]{2,1,0:T(8,128)(2,1)S(1)} collective-permute-done((bf16[1,64,1024]{2,1,0:T(8,128)(2,1)S(1)}, bf16[1,64,1024]{2,1,0:T(8,128)(2,1)S(1)}, u32[]{:S(2)}, u32[]{:S(2)}) %collective-permute-start.16) | collective-permute-done | bytes 131104 | tf_op jit(solution)/shard_map/ppermute | solution.py:656
  52.4 1.8 %collective-permute-start.15 = (bf16[1,64,1024]{2,1,0:T(8,128)(2,1)S(1)}, bf16[1,64,1024]{2,1,0:T(8,128)(2,1)S(1)}, u32[]{:S(2)}, u32[]{:S(2)}) collective-permute-start(bf16[1,64,1024]{2,1,0:T(8,128)(2,1)S(1)} %get-tuple-element.44.refs_0_), channel_id=1, source_target_pairs={{0,24},{8,16},{16,8},{24,0},{1,25},{9,17},{17,9},{25,1},{2,26},{10... | collective-permute-start | bytes 393224 | tf_op jit(solution)/shard_map/ppermute | solution.py:656
  54.2 12.5 %collective-permute-start.14 = (bf16[1,64,1024]{2,1,0:T(8,128)(2,1)S(1)}, bf16[1,64,1024]{2,1,0:T(8,128)(2,1)S(1)}, u32[]{:S(2)}, u32[]{:S(2)}) collective-permute-start(bf16[1,64,1024]{2,1,0:T(8,128)(2,1)S(1)} %get-tuple-element.44.refs_0_), channel_id=1, source_target_pairs={{0,16},{8,24},{16,0},{24,8},{1,17},{9,25},{17,1},{25,9},{2,18},{10... | collective-permute-start | bytes 393224 | tf_op jit(solution)/shard_map/ppermute | solution.py:656
  66.7 4.9 %collective-permute-done.10.refs_2_ = bf16[2,64,1024]{2,1,0:T(8,128)(2,1)S(1)} collective-permute-done((bf16[2,64,1024]{2,1,0:T(8,128)(2,1)S(1)}, bf16[2,64,1024]{2,1,0:T(8,128)(2,1)S(1)}, u32[]{:S(2)}, u32[]{:S(2)}) %collective-permute-start.10) | collective-permute-done | bytes 262176 | tf_op jit(solution)/shard_map/ppermute | solution.py:656
  71.7 6.3 %collective-permute-done.12.refs_5_ = bf16[2,64,1024]{2,1,0:T(8,128)(2,1)S(1)} collective-permute-done((bf16[2,64,1024]{2,1,0:T(8,128)(2,1)S(1)}, bf16[2,64,1024]{2,1,0:T(8,128)(2,1)S(1)}, u32[]{:S(2)}, u32[]{:S(2)}) %collective-permute-start.12) | collective-permute-done | bytes 262176 | tf_op jit(solution)/shard_map/ppermute | solution.py:656
  78.0 6.4 %join_early.1 = (bf16[2,256,1024]{2,1,0:T(8,128)(2,1)S(1)}, f32[256,2048]{1,0:T(8,128)S(1)}, bf16[1024,2048]{1,0:T(8,128)(2,1)S(1)}) custom-call(s32[4]{0:T(128)S(1)} %copy-done.3, bf16[2,128,1024]{2,1,0:T(8,128)(2,1)S(1)} %get-tuple-element.40.refs_0_, bf16[2,128,1024]{2,1,0:T(8,128)(2,1)S(1)} %collective-permute-done.9.refs_1_, ...), custom_call_target="tpu_custom_call" | custom-call | flops 2147483648 | bytes 8388608 | tf_op jit(solution)/shard_map/join_early/pallas_call | solution.py:401
  86.6 2.1 %join_late.1 = (bf16[1,256,1024]{2,1,0:T(8,128)(2,1)S(1)}, f32[128,2048]{1,0:T(8,128)S(1)}, bf16[128,2048]{1,0:T(8,128)(2,1)S(1)}) custom-call(s32[4]{0:T(128)S(1)} %copy-done.3, bf16[1,64,1024]{2,1,0:T(8,128)(2,1)S(1)} %get-tuple-element.44.refs_0_, bf16[1,64,1024]{2,1,0:T(8,128)(2,1)S(1)} %collective-permute-done.13.refs_1_, ...), custom_call_target="tpu_custom_call" | custom-call | flops 1073741824 | bytes 4194304 | tf_op jit(solution)/shard_map/join_late/pallas_call | solution.py:401
  95.6 2.1 %add_convert_fusion = (bf16[2,192,1024]{2,1,0:T(8,128)(2,1)S(1)}, bf16[2,192,1024]{2,1,0:T(8,128)(2,1)S(1)}) fusion(bf16[4,384,1024]{2,1,0:T(8,128)(2,1)} %collective-permute-done.4, bf16[4,384,1024]{2,1,0:T(8,128)(2,1)S(1)} %copy-done.4), kind=kLoop, calls=%fused_computation.2 | loop fusion | flops 3145728 | bytes 4718592 | tf_op jit(solution)/shard_map/convert_element_type | solution.py:720
  101.2 3.9 %collective-permute-done.25.refs_3_ = bf16[64,2048]{1,0:T(8,128)(2,1)S(1)} collective-permute-done((bf16[64,2048]{1,0:T(8,128)(2,1)S(1)}, bf16[64,2048]{1,0:T(8,128)(2,1)S(1)}, u32[]{:S(2)}, u32[]{:S(2)}) %collective-permute-start.25) | collective-permute-done | bytes 262176 | tf_op jit(solution)/shard_map/ppermute | solution.py:653
  105.9 3.4 %goals.1 = (bf16[128,2048]{1,0:T(8,128)(2,1)S(1)}, bf16[128,2048]{1,0:T(8,128)(2,1)S(1)}) custom-call(s32[4]{0:T(128)S(1)} %copy-done.3, s32[4,512]{1,0:T(4,128)S(1)} %copy-done.2, bf16[64,2048]{1,0:T(8,128)(2,1)} %refs_0_.1, bf16[64,2048]{1,0:T(8,128)(2,1)} %copy-done.8, bf16[64,2048]{1,0:T(8,128)(2,1)} %copy-done.7, bf16[64,2048]{1,0:T(8,128)(2,1)} %copy-done.9), custom_call_target="tpu_custom_call" | custom-call | flops 268435456 | bytes 2097152 | tf_op jit(solution)/shard_map/goals/pallas_call | solution.py:463
  113.1 19.4 %collective-permute-done.22.refs_3_ = bf16[128,1024]{1,0:T(8,128)(2,1)S(1)} collective-permute-done((bf16[128,1024]{1,0:T(8,128)(2,1)S(1)}, bf16[128,1024]{1,0:T(8,128)(2,1)S(1)}, u32[]{:S(2)}, u32[]{:S(2)}) %collective-permute-start.22) | collective-permute-done | bytes 262176 | tf_op jit(solution)/shard_map/ppermute | solution.py:653
  133.0 2.6 %collective-permute-start.29 = (f32[8,128]{1,0:T(8,128)S(1)}, f32[8,128]{1,0:T(8,128)S(1)}, u32[]{:S(2)}, u32[]{:S(2)}) collective-permute-start(f32[8,128]{1,0:T(8,128)S(1)} %get-tuple-element.55.refs_0_), channel_id=1, source_target_pairs={{0,24},{8,16},{16,8},{24,0},{1,25},{9,17},{17,9},{25,1},{2,26},{10... | collective-permute-start | bytes 12296 | tf_op jit(solution)/shard_map/ppermute | solution.py:656
  138.4 1.7 %collective-permute-done.28.refs_2_ = f32[8,128]{1,0:T(8,128)S(1)} collective-permute-done((f32[8,128]{1,0:T(8,128)S(1)}, f32[8,128]{1,0:T(8,128)S(1)}, u32[]{:S(2)}, u32[]{:S(2)}) %collective-permute-start.28) | collective-permute-done | bytes 4128 | tf_op jit(solution)/shard_map/ppermute | solution.py:656
  141.4 1.6 add_convert_fusion.2
  146.6 7.9 %collective-permute-done.8.refs_3_ = bf16[1,192,1024]{2,1,0:T(8,128)(2,1)S(1)} collective-permute-done((bf16[1,192,1024]{2,1,0:T(8,128)(2,1)S(1)}, bf16[1,192,1024]{2,1,0:T(8,128)(2,1)S(1)}, u32[]{:S(2)}, u32[]{:S(2)}) %collective-permute-start.8) | collective-permute-done | bytes 393248 | tf_op jit(solution)/shard_map/ppermute | solution.py:653
  155.8 9.8 %finish.1 = (bf16[512,1024]{1,0:T(8,128)(2,1)}, f32[3,1024,2048]{2,1,0:T(8,128)}) custom-call(s32[4,512]{1,0:T(4,128)S(1)} %copy-done.1, bf16[128,1024]{1,0:T(8,128)(2,1)S(1)} %bitcast.12, f32[384,1024]{1,0:T(8,128)S(1)} %convert_add_fusion.base_ref, bf16[2,192,1024]{2,1,0:T(8,128)(2,1)S(1)} %collective-permute-done.5.refs_0_, ...), custom_call_target="tpu_custom_call" | custom-call | flops 3221225472 | bytes 25165824 | tf_op jit(solution)/shard_map/finish/pallas_call | solution.py:604
  (78 shorter events, 34.1 us)
Async XLA Ops:
  8.9 16.4 %collective-permute-start = (bf16[4,128,1024]{2,1,0:T(8,128)(2,1)}, bf16[4,128,1024]{2,1,0:T(8,128)(2,1)S(1)}, u32[]{:S(2)}, u32[]{:S(2)}) collective-permute-start(bf16[4,128,1024]{2,1,0:T(8,128)(2,1)} %get-tuple-element.30), channel_id=1, source_target_pairs={{0,1},{1,0},{2,3},{3,2},{4,5},{5,4},{6,7},{7,6},{8,9},{9,8},{10,11... | collective-permute-start | bytes 3145736 | tf_op jit(solution)/shard_map/ppermute | solution.py:653
  20.2 73.9 %collective-permute-start.4 = (bf16[4,384,1024]{2,1,0:T(8,128)(2,1)}, bf16[4,384,1024]{2,1,0:T(8,128)(2,1)}, u32[]{:S(2)}, u32[]{:S(2)}) collective-permute-start(bf16[4,384,1024]{2,1,0:T(8,128)(2,1)} %get-tuple-element.39), channel_id=1, source_target_pairs={{0,1},{1,0},{2,3},{3,2},{4,5},{5,4},{6,7},{7,6},{8,9},{9,8},{10,11... | collective-permute-start | bytes 9437192 | tf_op jit(solution)/shard_map/ppermute | solution.py:653
  22.2 21.3 %collective-permute-start.9 = (bf16[2,128,1024]{2,1,0:T(8,128)(2,1)S(1)}, bf16[2,128,1024]{2,1,0:T(8,128)(2,1)S(1)}, u32[]{:S(2)}, u32[]{:S(2)}) collective-permute-start(bf16[2,128,1024]{2,1,0:T(8,128)(2,1)S(1)} %get-tuple-element.40.refs_0_), channel_id=1, source_target_pairs={{0,8},{8,0},{16,24},{24,16},{1,9},{9,1},{17,25},{25,17},{2,10},{10... | collective-permute-start | bytes 1572872 | tf_op jit(solution)/shard_map/ppermute | solution.py:656
  25.6 9.2 %collective-permute-start.1 = (bf16[128,1024]{1,0:T(8,128)(2,1)S(1)}, bf16[128,1024]{1,0:T(8,128)(2,1)S(1)}, u32[]{:S(2)}, u32[]{:S(2)}) collective-permute-start(bf16[128,1024]{1,0:T(8,128)(2,1)S(1)} %get-tuple-element.32), channel_id=1, source_target_pairs={{0,2},{1,3},{2,0},{3,1},{4,6},{5,7},{6,4},{7,5},{8,10},{9,11},{10,... | collective-permute-start | bytes 786440 | tf_op jit(solution)/shard_map/ppermute | solution.py:653
  27.1 13.1 %collective-permute-start.2 = (bf16[128,1024]{1,0:T(8,128)(2,1)S(1)}, bf16[128,1024]{1,0:T(8,128)(2,1)S(1)}, u32[]{:S(2)}, u32[]{:S(2)}) collective-permute-start(bf16[128,1024]{1,0:T(8,128)(2,1)S(1)} %get-tuple-element.33), channel_id=1, source_target_pairs={{0,6},{1,7},{2,4},{3,5},{4,2},{5,3},{6,0},{7,1},{8,14},{9,15},{10,... | collective-permute-start | bytes 786440 | tf_op jit(solution)/shard_map/ppermute | solution.py:653
  28.6 14.2 %collective-permute-start.3 = (bf16[128,1024]{1,0:T(8,128)(2,1)S(1)}, bf16[128,1024]{1,0:T(8,128)(2,1)S(1)}, u32[]{:S(2)}, u32[]{:S(2)}) collective-permute-start(bf16[128,1024]{1,0:T(8,128)(2,1)S(1)} %get-tuple-element.34), channel_id=1, source_target_pairs={{0,4},{1,5},{2,6},{3,7},{4,0},{5,1},{6,2},{7,3},{8,12},{9,13},{10,... | collective-permute-start | bytes 786440 | tf_op jit(solution)/shard_map/ppermute | solution.py:653
  34.8 19.4 %collective-permute-start.11 = (bf16[2,64,1024]{2,1,0:T(8,128)(2,1)S(1)}, bf16[2,64,1024]{2,1,0:T(8,128)(2,1)S(1)}, u32[]{:S(2)}, u32[]{:S(2)}) collective-permute-start(bf16[2,64,1024]{2,1,0:T(8,128)(2,1)S(1)} %get-tuple-element.41), channel_id=1, source_target_pairs={{0,24},{8,16},{16,8},{24,0},{1,25},{9,17},{17,9},{25,1},{2,26},{10... | collective-permute-start | bytes 786440 | tf_op jit(solution)/shard_map/ppermute | solution.py:656
  40.3 31.3 %collective-permute-start.10 = (bf16[2,64,1024]{2,1,0:T(8,128)(2,1)S(1)}, bf16[2,64,1024]{2,1,0:T(8,128)(2,1)S(1)}, u32[]{:S(2)}, u32[]{:S(2)}) collective-permute-start(bf16[2,64,1024]{2,1,0:T(8,128)(2,1)S(1)} %get-tuple-element.41), channel_id=1, source_target_pairs={{0,16},{8,24},{16,0},{24,8},{1,17},{9,25},{17,1},{25,9},{2,18},{10... | collective-permute-start | bytes 786440 | tf_op jit(solution)/shard_map/ppermute | solution.py:656
  43.0 9.4 %collective-permute-start.16 = (bf16[1,64,1024]{2,1,0:T(8,128)(2,1)S(1)}, bf16[1,64,1024]{2,1,0:T(8,128)(2,1)S(1)}, u32[]{:S(2)}, u32[]{:S(2)}) collective-permute-start(bf16[1,64,1024]{2,1,0:T(8,128)(2,1)S(1)} %get-tuple-element.45), channel_id=1, source_target_pairs={{0,8},{8,0},{16,24},{24,16},{1,9},{9,1},{17,25},{25,17},{2,10},{10... | collective-permute-start | bytes 393224 | tf_op jit(solution)/shard_map/ppermute | solution.py:656
  43.5 34.5 %collective-permute-start.12 = (bf16[2,64,1024]{2,1,0:T(8,128)(2,1)S(1)}, bf16[2,64,1024]{2,1,0:T(8,128)(2,1)S(1)}, u32[]{:S(2)}, u32[]{:S(2)}) collective-permute-start(bf16[2,64,1024]{2,1,0:T(8,128)(2,1)S(1)} %slice_select_fusion.refs_4_), channel_id=1, source_target_pairs={{0,16},{8,24},{16,0},{24,8},{1,17},{9,25},{17,1},{25,9},{2,18},{10... | collective-permute-start | bytes 786440 | tf_op jit(solution)/shard_map/ppermute | solution.py:656
  52.4 32.0 %collective-permute-start.15 = (bf16[1,64,1024]{2,1,0:T(8,128)(2,1)S(1)}, bf16[1,64,1024]{2,1,0:T(8,128)(2,1)S(1)}, u32[]{:S(2)}, u32[]{:S(2)}) collective-permute-start(bf16[1,64,1024]{2,1,0:T(8,128)(2,1)S(1)} %get-tuple-element.44.refs_0_), channel_id=1, source_target_pairs={{0,24},{8,16},{16,8},{24,0},{1,25},{9,17},{17,9},{25,1},{2,26},{10... | collective-permute-start | bytes 393224 | tf_op jit(solution)/shard_map/ppermute | solution.py:656
  54.2 30.9 %collective-permute-start.14 = (bf16[1,64,1024]{2,1,0:T(8,128)(2,1)S(1)}, bf16[1,64,1024]{2,1,0:T(8,128)(2,1)S(1)}, u32[]{:S(2)}, u32[]{:S(2)}) collective-permute-start(bf16[1,64,1024]{2,1,0:T(8,128)(2,1)S(1)} %get-tuple-element.44.refs_0_), channel_id=1, source_target_pairs={{0,16},{8,24},{16,0},{24,8},{1,17},{9,25},{17,1},{25,9},{2,18},{10... | collective-permute-start | bytes 393224 | tf_op jit(solution)/shard_map/ppermute | solution.py:656
  71.6 13.5 %collective-permute-start.13 = (bf16[1,64,1024]{2,1,0:T(8,128)(2,1)S(1)}, bf16[1,64,1024]{2,1,0:T(8,128)(2,1)S(1)}, u32[]{:S(2)}, u32[]{:S(2)}) collective-permute-start(bf16[1,64,1024]{2,1,0:T(8,128)(2,1)S(1)} %get-tuple-element.44.refs_0_), channel_id=1, source_target_pairs={{0,8},{8,0},{16,24},{24,16},{1,9},{9,1},{17,25},{25,17},{2,10},{10... | collective-permute-start | bytes 393224 | tf_op jit(solution)/shard_map/ppermute | solution.py:656
  88.8 9.4 %collective-permute-start.24 = (bf16[64,2048]{1,0:T(8,128)(2,1)S(1)}, bf16[64,2048]{1,0:T(8,128)(2,1)S(1)}, u32[]{:S(2)}, u32[]{:S(2)}) collective-permute-start(bf16[64,2048]{1,0:T(8,128)(2,1)S(1)} %copy-done.6), channel_id=1, source_target_pairs={{0,4},{1,5},{2,6},{3,7},{4,0},{5,1},{6,2},{7,3},{8,12},{9,13},{10,... | collective-permute-start | bytes 786440 | tf_op jit(solution)/shard_map/ppermute | solution.py:653
  90.3 9.4 %collective-permute-start.23 = (bf16[64,2048]{1,0:T(8,128)(2,1)S(1)}, bf16[64,2048]{1,0:T(8,128)(2,1)S(1)}, u32[]{:S(2)}, u32[]{:S(2)}) collective-permute-start(bf16[64,2048]{1,0:T(8,128)(2,1)S(1)} %copy-done.6), channel_id=1, source_target_pairs={{0,2},{1,3},{2,0},{3,1},{4,6},{5,7},{6,4},{7,5},{8,10},{9,11},{10,... | collective-permute-start | bytes 786440 | tf_op jit(solution)/shard_map/ppermute | solution.py:653
  91.8 13.3 %collective-permute-start.25 = (bf16[64,2048]{1,0:T(8,128)(2,1)S(1)}, bf16[64,2048]{1,0:T(8,128)(2,1)S(1)}, u32[]{:S(2)}, u32[]{:S(2)}) collective-permute-start(bf16[64,2048]{1,0:T(8,128)(2,1)S(1)} %copy-done.6), channel_id=1, source_target_pairs={{0,6},{1,7},{2,4},{3,5},{4,2},{5,3},{6,0},{7,1},{8,14},{9,15},{10,... | collective-permute-start | bytes 786440 | tf_op jit(solution)/shard_map/ppermute | solution.py:653
  92.5 16.8 %collective-permute-start.20 = (bf16[128,1024]{1,0:T(8,128)(2,1)S(1)}, bf16[128,1024]{1,0:T(8,128)(2,1)S(1)}, u32[]{:S(2)}, u32[]{:S(2)}) collective-permute-start(bf16[128,1024]{1,0:T(8,128)(2,1)S(1)} %get-tuple-element.66), channel_id=1, source_target_pairs={{0,4},{1,5},{2,6},{3,7},{4,0},{5,1},{6,2},{7,3},{8,12},{9,13},{10,... | collective-permute-start | bytes 786440 | tf_op jit(solution)/shard_map/ppermute | solution.py:653
  94.1 16.7 %collective-permute-start.19 = (bf16[128,1024]{1,0:T(8,128)(2,1)S(1)}, bf16[128,1024]{1,0:T(8,128)(2,1)S(1)}, u32[]{:S(2)}, u32[]{:S(2)}) collective-permute-start(bf16[128,1024]{1,0:T(8,128)(2,1)S(1)} %get-tuple-element.67), channel_id=1, source_target_pairs={{0,2},{1,3},{2,0},{3,1},{4,6},{5,7},{6,4},{7,5},{8,10},{9,11},{10,... | collective-permute-start | bytes 786440 | tf_op jit(solution)/shard_map/ppermute | solution.py:653
  98.2 43.2 %collective-permute-start.7 = (bf16[2,192,1024]{2,1,0:T(8,128)(2,1)S(1)}, bf16[2,192,1024]{2,1,0:T(8,128)(2,1)S(1)}, u32[]{:S(2)}, u32[]{:S(2)}) collective-permute-start(bf16[2,192,1024]{2,1,0:T(8,128)(2,1)S(1)} %get-tuple-element.62), channel_id=1, source_target_pairs={{0,4},{1,5},{2,6},{3,7},{4,0},{5,1},{6,2},{7,3},{8,12},{9,13},{10,... | collective-permute-start | bytes 2359304 | tf_op jit(solution)/shard_map/ppermute | solution.py:653
  99.7 41.7 %collective-permute-start.5 = (bf16[2,192,1024]{2,1,0:T(8,128)(2,1)S(1)}, bf16[2,192,1024]{2,1,0:T(8,128)(2,1)S(1)}, u32[]{:S(2)}, u32[]{:S(2)}) collective-permute-start(bf16[2,192,1024]{2,1,0:T(8,128)(2,1)S(1)} %get-tuple-element.63), channel_id=1, source_target_pairs={{0,2},{1,3},{2,0},{3,1},{4,6},{5,7},{6,4},{7,5},{8,10},{9,11},{10,... | collective-permute-start | bytes 2359304 | tf_op jit(solution)/shard_map/ppermute | solution.py:653
  111.0 21.5 %collective-permute-start.22 = (bf16[128,1024]{1,0:T(8,128)(2,1)S(1)}, bf16[128,1024]{1,0:T(8,128)(2,1)S(1)}, u32[]{:S(2)}, u32[]{:S(2)}) collective-permute-start(bf16[128,1024]{1,0:T(8,128)(2,1)S(1)} %get-tuple-element.56), channel_id=1, source_target_pairs={{0,2},{1,3},{2,0},{3,1},{4,6},{5,7},{6,4},{7,5},{8,10},{9,11},{10,... | collective-permute-start | bytes 786440 | tf_op jit(solution)/shard_map/ppermute | solution.py:653
  112.6 19.9 %collective-permute-start.21 = (bf16[128,1024]{1,0:T(8,128)(2,1)S(1)}, bf16[128,1024]{1,0:T(8,128)(2,1)S(1)}, u32[]{:S(2)}, u32[]{:S(2)}) collective-permute-start(bf16[128,1024]{1,0:T(8,128)(2,1)S(1)} %get-tuple-element.64), channel_id=1, source_target_pairs={{0,4},{1,5},{2,6},{3,7},{4,0},{5,1},{6,2},{7,3},{8,12},{9,13},{10,... | collective-permute-start | bytes 786440 | tf_op jit(solution)/shard_map/ppermute | solution.py:653
  143.0 11.5 %collective-permute-start.8 = (bf16[1,192,1024]{2,1,0:T(8,128)(2,1)S(1)}, bf16[1,192,1024]{2,1,0:T(8,128)(2,1)S(1)}, u32[]{:S(2)}, u32[]{:S(2)}) collective-permute-start(bf16[1,192,1024]{2,1,0:T(8,128)(2,1)S(1)} %get-tuple-element.60), channel_id=1, source_target_pairs={{0,2},{1,3},{2,0},{3,1},{4,6},{5,7},{6,4},{7,5},{8,10},{9,11},{10,... | collective-permute-start | bytes 1179656 | tf_op jit(solution)/shard_map/ppermute | solution.py:653
  144.6 11.2 %collective-permute-start.6 = (bf16[1,192,1024]{2,1,0:T(8,128)(2,1)S(1)}, bf16[1,192,1024]{2,1,0:T(8,128)(2,1)S(1)}, u32[]{:S(2)}, u32[]{:S(2)}) collective-permute-start(bf16[1,192,1024]{2,1,0:T(8,128)(2,1)S(1)} %get-tuple-element.61), channel_id=1, source_target_pairs={{0,4},{1,5},{2,6},{3,7},{4,0},{5,1},{6,2},{7,3},{8,12},{9,13},{10,... | collective-permute-start | bytes 1179656 | tf_op jit(solution)/shard_map/ppermute | solution.py:653
  (17 other events, 125.6 us)
